TPU v7x, 32 devices: a whole 2x2x4 slice. The times are simulated.
32 devices in a mesh: groups: 2 (over x), rows: 16 (over z, y, core).
Axes of the slice: x: 2, y: 2, z: 4, core: 2. Of those that a mesh axis runs over, the one named last changes fastest.
Arguments:
- points: bfloat16 [64, 32768], P(None, ('groups', 'rows')), parts along dimension 1, may hold values from -12 to 12
- landmarks: bfloat16 [64, 2048], P(None, 'groups'), parts along dimension 1, may hold values from -12 to 12
- chol: float32 [2048, 1024], P('groups'), parts along dimension 0
- ridge: float32 [2], P('groups'), parts along dimension 0, may hold values from 0.5 to 2
- solution: float32 [8, 32768], P(None, ('groups', 'rows')), parts along dimension 1, may hold values from -6 to 6
- residual: float32 [8, 32768], P(None, ('groups', 'rows')), parts along dimension 1, may hold values from -6 to 6
- direction: float32 [8, 32768], P(None, ('groups', 'rows')), parts along dimension 1, may hold values from -6 to 6
- rz_prev: float32 [16], P('groups'), parts along dimension 0, may hold values from 8192 to 32768
Outputs:
- solution_new: float32 [8, 32768], P(None, ('groups', 'rows')), parts along dimension 1
- residual_new: float32 [8, 32768], P(None, ('groups', 'rows')), parts along dimension 1
- direction_new: float32 [8, 32768], P(None, ('groups', 'rows')), parts along dimension 1
- inner_new: float32 [16], P('groups'), parts along dimension 0
There are 2 independent parts, one for each index of `groups`. A program takes and returns all parts, laid end to end along the dimension named above; each array names one. Nothing has to cross between parts.
All inputs are finite; a program needn't handle non-finite values.
Results may differ from a plain program's by a relative error of at most 0.0064.
Values may be sent and summed in bfloat16 or wider, within the bound.
A program may use at most 64 MiB of HBM per device.

v0:
```python
import functools
import math

import jax
import jax.numpy as jnp
from jax import lax
from jax.experimental import pallas as pl
from jax.experimental.pallas import tpu as pltpu
from jax.sharding import PartitionSpec as P

HIGH = lax.Precision.HIGHEST
TILE = 128
CHUNK = 256
GROUP = 2 * TILE
STORED_BLOCKS = 16


def dot_nn(left, right, precision=None):
    return lax.dot_general(
        left, right, (((1,), (0,)), ((), ())), precision=precision, preferred_element_type=jnp.float32
    )


def dot_nt(left, right, precision=None):
    return lax.dot_general(
        left, right, (((1,), (1,)), ((), ())), precision=precision, preferred_element_type=jnp.float32
    )


def dot_tn(left, right):
    return lax.dot_general(
        left, right, (((0,), (0,)), ((), ())), preferred_element_type=jnp.float32
    )


def split(values):
    top = values.astype(jnp.bfloat16).astype(jnp.float32)
    rest = values - top
    mid = rest.astype(jnp.bfloat16).astype(jnp.float32)
    return top, mid, rest - mid


def store_split(ref, at, values):
    for term, part in enumerate(split(values)):
        ref[(term,) + at] = part.astype(jnp.bfloat16)


def dot_split(left, parts, dot):
    outs = left.shape[0]
    stacked = jnp.concatenate(split(left), axis=0).astype(jnp.bfloat16)
    high = dot(stacked, parts[0])
    mid = dot(stacked[:2 * outs], parts[1])
    low = dot(stacked[:2 * outs], parts[2])
    small = low[:outs] + mid[outs:] + high[2 * outs:]
    return high[:outs] + (high[outs:2 * outs] + mid[:outs] + small)


def norm_rows(features, first):
    wide = features.astype(jnp.float32)
    half = -0.5 * jnp.sum(wide * wide, axis=0, keepdims=True)
    top = half.astype(jnp.bfloat16).astype(jnp.float32)
    rest = half - top
    mid = rest.astype(jnp.bfloat16).astype(jnp.float32)
    low = rest - mid
    row = lax.broadcasted_iota(jnp.int32, (16, features.shape[1]), 0)
    at = 0 if first else 3
    ones = 3 - at
    rows = jnp.where((row >= ones) & (row < ones + 3), 1.0, 0.0)
    rows = jnp.where(row == at, top, rows)
    rows = jnp.where(row == at + 1, mid, rows)
    rows = jnp.where(row == at + 2, low, rows)
    return rows.astype(jnp.bfloat16)


def eye_mask(width):
    shape = (8, width)
    return lax.broadcasted_iota(jnp.int32, shape, 0) == lax.broadcasted_iota(jnp.int32, shape, 1)


def to_row(column, width):
    return jnp.sum(jnp.where(eye_mask(width), column, 0.0), axis=0, keepdims=True)


def to_column(row):
    return jnp.sum(jnp.where(eye_mask(row.shape[1]), row, 0.0), axis=1, keepdims=True)


def kernel(
    n,
    keep,
    points_ref,
    landmarks_ref,
    chol_hbm,
    ridge_ref,
    residual_ref,
    direction_ref,
    rz_ref,
    image_out,
    direction_out,
    inner_out,
    alpha_out,
    chol,
    chol_parts,
    inverse_parts,
    inverse,
    points,
    own_aug,
    col_aug,
    cross_t,
    kernel_store,
    rs_send,
    rs_recv,
    ag,
    proj,
    work,
    inner_buf,
    dirs,
    curv_buf,
    chol_sem,
    rs_sems,
    ag_sems,
    inner_sems,
    dir_sems,
    curv_sems,
    point_recv,
    point_fwd,
    point_side,
    point_back,
    share_sems,
):
    me = lax.axis_index("rows")
    feat, local = points_ref.shape
    land = landmarks_ref.shape[1]
    outs = residual_ref.shape[0]
    chips = n // 2
    half = chips // 2
    core = me % 2
    chip = me // 2
    odd = chip % 2
    pos = (1 - odd) * (chip // 2) + odd * (chips - (chip + 1) // 2)
    scale = math.log2(math.e) / feat

    def row_of(position, lane):
        position = (position + chips) % chips
        upper = position // half
        at = (1 - upper) * (2 * position) + upper * (2 * chips - 1 - 2 * position)
        return at * 2 + (core + lane) % 2

    def remote(src, dst, send, recv, to):
        return pltpu.make_async_remote_copy(
            src_ref=src,
            dst_ref=dst,
            send_sem=send,
            recv_sem=recv,
            device_id={"rows": to},
            device_id_type=pl.DeviceIdType.MESH,
        )

    def others(body):
        lax.fori_loop(1, n, lambda k, carry: (body((me + k) % n), carry)[1], 0)

    def send_all(src_of, buf, sems):
        others(lambda to: remote(src_of(to), buf.at[me], sems.at[0, to], sems.at[1, me], to).start())

    def wait_all(src_of, buf, sems):
        others(lambda to: remote(src_of(to), buf.at[to], sems.at[0, to], sems.at[1, to], to).wait_recv())

    def drain(src_of, buf, sems):
        others(lambda to: remote(src_of(to), buf.at[me], sems.at[0, to], sems.at[1, me], to).wait_send())

    chol_copy = pltpu.make_async_copy(chol_hbm, chol, chol_sem)
    chol_copy.start()

    barrier = pltpu.get_barrier_semaphore()
    others(lambda to: pl.semaphore_signal(
        barrier, inc=1, device_id={"rows": to}, device_id_type=pl.DeviceIdType.MESH))

    right = row_of(pos + 1, 0)
    left = row_of(pos - 1, 0)
    partner = row_of(pos, 1)
    own_slot = points.at[me]
    first_right = remote(points_ref, own_slot, point_fwd.at[me], point_recv.at[me], right)
    first_left = remote(points_ref, own_slot, point_back, point_recv.at[me], left)
    first_side = remote(points_ref, own_slot, point_side.at[me], point_recv.at[me], partner)

    own_aug[0:feat, :] = points_ref[...]
    own_aug[feat:, :] = norm_rows(points_ref[...], True)
    col_aug[0:feat, :] = landmarks_ref[...]
    col_aug[feat:, :] = norm_rows(landmarks_ref[...], False)

    def entries(left_aug, at, right_aug):
        return jnp.exp2(dot_tn(left_aug[:, pl.ds(at, CHUNK)], right_aug[...]) * scale)

    proj[...] = jnp.zeros_like(proj)

    def project(i, carry):
        at = pl.multiple_of(i * CHUNK, CHUNK)
        parts = [part.astype(jnp.bfloat16) for part in split(entries(own_aug, at, col_aug))]
        proj[...] += dot_split(residual_ref[:, pl.ds(at, CHUNK)], parts, dot_nn)
        return carry

    lax.fori_loop(0, local // CHUNK, project, 0)

    pl.semaphore_wait(barrier, n - 1)

    tiles = land // TILE
    groups = land // GROUP
    rows_per = outs * tiles // n
    for piece in range(n):
        h, j = piece // tiles, piece % tiles
        rs_send[piece] = proj[h * rows_per:(h + 1) * rows_per, j * TILE:(j + 1) * TILE]
    send_all(lambda to: rs_send.at[to], rs_recv, rs_sems)
    rs_recv[me] = rs_send[me]
    first_right.start()
    first_left.start()
    first_side.start()

    def landmark_rows(i, carry):
        at = pl.multiple_of(i * CHUNK, CHUNK)
        store_split(cross_t, (pl.ds(at, CHUNK), slice(None)), entries(col_aug, at, own_aug))
        return carry

    lax.fori_loop(0, land // CHUNK, landmark_rows, 0)

    def make_block(owner, slot):
        col_aug[0:feat, :] = points[owner]
        col_aug[feat:, :] = norm_rows(points[owner], False)

        for at in range(0, local, CHUNK):
            kernel_store[slot, at:at + CHUNK, :] = entries(col_aug, at, own_aug).astype(jnp.bfloat16)

    own_points = pltpu.make_async_copy(points_ref, own_slot, chol_sem)
    chol_copy.wait()
    own_points.start()
    own_points.wait()

    row = lax.broadcasted_iota(jnp.int32, (TILE, TILE), 0)
    col = lax.broadcasted_iota(jnp.int32, (TILE, TILE), 1)

    share = tiles // 2
    first = core * share

    def own_block(b):
        at = pl.multiple_of((first + b) * TILE, TILE)
        return chol[pl.ds(at, TILE), pl.ds(at, TILE)]

    inverted = [jnp.where(row == col, 1.0 / own_block(b), 0.0) for b in range(share)]
    size = 1
    while size < TILE:
        below = (row // size == col // size + 1) & (row // (2 * size) == col // (2 * size))
        for b in range(share):
            off = jnp.where(below, own_block(b), 0.0)
            if size == 1:
                on_row = jnp.sum(inverted[b], axis=1, keepdims=True)
                on_col = jnp.sum(inverted[b], axis=0, keepdims=True)
                change = on_row * off * on_col
            else:
                change = dot_nn(dot_nn(inverted[b], off, HIGH), inverted[b], HIGH)
            inverted[b] = inverted[b] - change
        size *= 2
    for b in range(share):
        inverse[first + b] = inverted[b]

    wait_all(lambda to: rs_send.at[to], rs_recv, rs_sems)
    ag[me] = jnp.sum(rs_recv[...], axis=0)
    send_all(lambda to: ag.at[me], ag, ag_sems)

    shares = inverse.at[pl.ds(first, share)]
    shared = remote(shares, shares, share_sems.at[0], share_sems.at[1], partner)
    shared.start()

    def pass_on(s, both):
        near = row_of(pos - s, 0)
        remote(points_ref, points.at[near], point_fwd.at[near], point_recv.at[near], right).wait_recv()
        if both:
            remote(points.at[near], points.at[near], point_fwd.at[near], point_recv.at[near], right).start()
        remote(points.at[near], points.at[near], point_side.at[near], point_recv.at[near], partner).start()
        if both:
            far = row_of(pos + s, 0)
            remote(points_ref, points.at[far], point_fwd.at[far], point_recv.at[far], left).wait_recv()
            remote(points.at[far], points.at[far], point_side.at[far], point_recv.at[far], partner).start()

            @pl.when(s < half - 1)
            def _():
                remote(points.at[far], points.at[far], point_fwd.at[far], point_recv.at[far], left).start()

    def build_lanes(s, both):
        def build(lane):
            def one(way, carry):
                owner = row_of(pos - s + 2 * s * way, lane)
                if lane == 1:
                    remote(points_ref, points.at[owner], point_side.at[owner], point_recv.at[owner], partner).wait_recv()
                if keep:
                    make_block(owner, owner)
                return carry

            lax.fori_loop(0, 2 if both else 1, one, 0)

        build(0)
        build(1)

    pass_on(1, True)
    build_lanes(1, True)
    remote(points_ref, points.at[partner], point_side.at[partner], point_recv.at[partner], partner).wait_recv()

    other = inverse.at[pl.ds(share - first, share)]
    remote(other, other, share_sems.at[0], share_sems.at[1], partner).wait_recv()
    for b in range(groups):
        upper, lower = inverse[2 * b], inverse[2 * b + 1]
        at, end = b * GROUP, (b + 1) * GROUP
        off = chol[at + TILE:end, at:at + TILE]
        change = dot_nn(dot_nn(lower, off, HIGH), upper, HIGH)
        zero = jnp.zeros_like(upper)
        whole = jnp.concatenate(
            [jnp.concatenate([upper, zero], axis=1), jnp.concatenate([-change, lower], axis=1)], axis=0
        )
        store_split(inverse_parts, (b,), whole)
        if b > 0:
            store_split(chol_parts, (slice(at, end), slice(0, at)), chol[at:end, :at])

    pass_on(2, True)
    wait_all(lambda to: ag.at[me], ag, ag_sems)
    for piece in range(n):
        h, j = piece // tiles, piece % tiles
        work[h * rows_per:(h + 1) * rows_per, j * TILE:(j + 1) * TILE] = ag[piece]
    pieces = [work[:, b * GROUP:(b + 1) * GROUP] for b in range(groups)]

    def block_parts(i, j):
        rows, cols = slice(i * GROUP, (i + 1) * GROUP), slice(j * GROUP, (j + 1) * GROUP)
        return [chol_parts[term, rows, cols] for term in range(3)]

    def inverse_of(b):
        return [inverse_parts[term, b] for term in range(3)]

    for b in range(groups):
        pieces[b] = dot_split(pieces[b], inverse_of(b), dot_nt)
        for i in range(b + 1, groups):
            pieces[i] = pieces[i] - dot_split(pieces[b], block_parts(i, b), dot_nt)
    for b in reversed(range(groups)):
        pieces[b] = dot_split(pieces[b], inverse_of(b), dot_nn)
        for j in reversed(range(b)):
            pieces[j] = pieces[j] - dot_split(pieces[b], block_parts(b, j), dot_nn)
    coeffs = jnp.concatenate(pieces, axis=1)

    ridge = ridge_ref[0]
    residual = residual_ref[...]
    precond = (residual - dot_split(coeffs, [cross_t.at[term][...] for term in range(3)], dot_nn)) / ridge
    inner_buf[me] = to_row(jnp.sum(precond * residual, axis=1, keepdims=True), TILE)
    send_all(lambda to: inner_buf.at[me], inner_buf, inner_sems)

    pass_on(3, True)
    if keep:
        make_block(partner, partner)
    build_lanes(2, True)
    wait_all(lambda to: inner_buf.at[me], inner_buf, inner_sems)
    inner_row = jnp.sum(inner_buf[...], axis=0)
    inner_out[...] = inner_row[:, :outs]
    inner = to_column(inner_row)
    direction_new = precond + (inner / to_column(rz_ref[...])) * direction_ref[...]
    direction_out[...] = direction_new
    dirs[me] = direction_new.astype(jnp.bfloat16)
    send_all(lambda to: dirs.at[me], dirs, dir_sems)

    if keep:
        make_block(me, me)
    build_lanes(3, True)

    def later(s, carry):
        pass_on(s, True)
        build_lanes(s, True)
        return carry

    lax.fori_loop(4, half, later, 0)
    pass_on(half, False)
    build_lanes(half, False)

    def image_part(owner, slot):
        if not keep:
            make_block(owner, slot)
        proj[...] += dot_nn(dirs[owner], kernel_store[slot])

    proj[...] = jnp.zeros_like(proj)
    image_part(me, me if keep else 0)

    def gather_image(to):
        remote(dirs.at[me], dirs.at[to], dir_sems.at[0, to], dir_sems.at[1, to], to).wait_recv()
        image_part(to, to if keep else 0)

    others(gather_image)

    direction_new = direction_out[...]
    image = proj[...] + ridge * direction_new
    image_out[...] = image
    curv_buf[me] = to_row(jnp.sum(direction_new * image, axis=1, keepdims=True), TILE)
    send_all(lambda to: curv_buf.at[me], curv_buf, curv_sems)

    drain(lambda to: rs_send.at[to], rs_recv, rs_sems)
    drain(lambda to: ag.at[me], ag, ag_sems)
    drain(lambda to: inner_buf.at[me], inner_buf, inner_sems)
    drain(lambda to: dirs.at[me], dirs, dir_sems)
    shared.wait_send()
    first_right.wait_send()
    first_left.wait_send()
    first_side.wait_send()

    def relay_drain(s, both):
        near = row_of(pos - s, 0)
        remote(points.at[near], points.at[near], point_side.at[near], point_recv.at[near], partner).wait_send()
        if both:
            remote(points.at[near], points.at[near], point_fwd.at[near], point_recv.at[near], right).wait_send()
            far = row_of(pos + s, 0)
            remote(points.at[far], points.at[far], point_side.at[far], point_recv.at[far], partner).wait_send()

            @pl.when(s < half - 1)
            def _():
                remote(points.at[far], points.at[far], point_fwd.at[far], point_recv.at[far], left).wait_send()

    lax.fori_loop(1, half, lambda s, carry: (relay_drain(s, True), carry)[1], 0)
    relay_drain(half, False)

    wait_all(lambda to: curv_buf.at[me], curv_buf, curv_sems)
    alpha_out[...] = inner_out[...] / jnp.sum(curv_buf[...], axis=0)[:, :outs]
    drain(lambda to: curv_buf.at[me], curv_buf, curv_sems)


def finish(
    image_ref,
    direction_ref,
    inner_ref,
    alpha_ref,
    solution_ref,
    residual_ref,
    solution_out,
    residual_out,
    direction_out,
    inner_out,
):
    alpha = to_column(alpha_ref[...])
    direction = direction_ref[...]
    solution_out[...] = solution_ref[...] + alpha * direction
    residual_out[...] = residual_ref[...] - alpha * image_ref[...]
    direction_out[...] = direction
    inner_out[...] = inner_ref[...]


def solution(mesh):
    n = mesh.shape["rows"]

    def local(points, landmarks, chol, ridge, solution, residual, direction, rz_prev):
        feat, own = points.shape
        land = landmarks.shape[1]
        outs = residual.shape[0]
        keep = n <= STORED_BLOCKS
        piece = outs * land // (TILE * n)
        f32, bf16 = jnp.float32, jnp.bfloat16
        vmem = pl.BlockSpec(memory_space=pltpu.VMEM)
        wide = jax.ShapeDtypeStruct((outs, own), f32)
        thin = jax.ShapeDtypeStruct((1, outs), f32)
        dma = pltpu.SemaphoreType.DMA
        results = pl.pallas_call(
            functools.partial(kernel, n, keep),
            out_shape=(wide, wide, thin, thin),
            in_specs=[
                vmem,
                vmem,
                pl.BlockSpec(memory_space=pl.ANY),
                pl.BlockSpec(memory_space=pltpu.SMEM),
                vmem,
                vmem,
                vmem,
            ],
            out_specs=(vmem,) * 4,
            scratch_shapes=[
                pltpu.VMEM((land, land), f32),
                pltpu.VMEM((3, land, land), bf16),
                pltpu.VMEM((3, land // GROUP, GROUP, GROUP), bf16),
                pltpu.VMEM((land // TILE, TILE, TILE), f32),
                pltpu.VMEM((n, feat, own), bf16),
                pltpu.VMEM((feat + 16, own), bf16),
                pltpu.VMEM((feat + 16, own), bf16),
                pltpu.VMEM((3, land, own), bf16),
                pltpu.VMEM((n if keep else 1, own, own), bf16),
                pltpu.VMEM((n, piece, TILE), f32),
                pltpu.VMEM((n, piece, TILE), f32),
                pltpu.VMEM((n, piece, TILE), f32),
                pltpu.VMEM((outs, land), f32),
                pltpu.VMEM((outs, land), f32),
                pltpu.VMEM((n, 1, TILE), f32),
                pltpu.VMEM((n, outs, own), bf16),
                pltpu.VMEM((n, 1, TILE), f32),
                dma,
                dma((2, n)),
                dma((2, n)),
                dma((2, n)),
                dma((2, n)),
                dma((2, n)),
                dma((n,)),
                dma((n,)),
                dma((n,)),
                dma,
                dma((2,)),
            ],
            compiler_params=pltpu.CompilerParams(
                collective_id=0, has_side_effects=True, vmem_limit_bytes=62 * 1024 * 1024
            ),
            name="cg_step",
        )(points, landmarks, chol, ridge, residual, direction, rz_prev.reshape(1, outs))
        results = pl.pallas_call(
            finish,
            out_shape=(wide, wide, wide, thin),
            in_specs=[vmem] * 6,
            out_specs=(vmem,) * 4,
            name="finish",
        )(*results, solution, residual)
        return (results[0], results[1], results[2], results[3].reshape(outs))

    wide_spec = P(None, ("groups", "rows"))
    in_specs = (
        wide_spec,
        P(None, "groups"),
        P("groups", None),
        P("groups"),
        wide_spec,
        wide_spec,
        wide_spec,
        P("groups"),
    )
    out_specs = (wide_spec, wide_spec, wide_spec, P("groups"))
    return jax.shard_map(local, mesh=mesh, in_specs=in_specs, out_specs=out_specs, check_vma=False)
```

profile of v0, /device:TPU:0, one launch (start us, length us, event | category | flops | bytes accessed | tf_op | source)
XLA Modules:
  0.0 48.1 jit_solution(8279795752732260301)
XLA Ops:
  1.3 45.3 %cg_step.1 = (f32[8,1024]{1,0:T(8,128)}, f32[8,1024]{1,0:T(8,128)}, f32[1,8]{1,0:T(1,128)}, f32[1,8]{1,0:T(1,128)}) custom-call(bf16[64,1024]{1,0:T(8,128)(2,1)} %points_ref.1, bf16[64,1024]{1,0:T(8,128)(2,1)} %landmarks_ref.1, f32[1024,1024]{1,0:T(8,128)} %chol_hbm.1, f32[1]{0:T(128)S(6)} %copy.12.ridge_ref, f32[8,1024]{1,0:T(8,128)} %residual_ref.3, ...), custom_call_target="tpu_custom_call" | custom-call | tf_op jit(solution)/shard_map/cg_step/pallas_call | solution.py:460
  46.6 1.5 %finish.1 = (f32[8,1024]{1,0:T(8,128)}, f32[8,1024]{1,0:T(8,128)}, f32[8,1024]{1,0:T(8,128)}, f32[1,8]{1,0:T(1,128)}) custom-call(f32[8,1024]{1,0:T(8,128)} %get-tuple-element.12.image_ref, f32[8,1024]{1,0:T(8,128)} %get-tuple-element.13.direction_ref, f32[1,8]{1,0:T(1,128)} %get-tuple-element.14.inner_ref, f32[1,8]{1,0:T(1,128)} %get-tuple-element.15.alpha_ref, ...), custom_call_target="tpu_custom_call" | custom-call | tf_op jit(solution)/shard_map/finish/pallas_call | solution.py:508
where the time goes:
time: 48.3 us; the launch traced here: 48.1 us
  Pallas kernels  46.8 us (97%)
  between operations  1.29 us (3%)
    pallas_call x1, Pallas kernels, local(): pl.pallas_call(functools.partial(kernel, n, keep), out_shape=(wide, wide,...  45.3 us
    pallas_call x1, Pallas kernels, local(): pl.pallas_call(finish, out_shape=(wide, wide, wide, thin), in_specs=[vmem...  1.54 us

commit v1 on v0

--- a/solution.py
+++ b/solution.py
@@ -105,27 +105,31 @@
     inverse,
     points,
     own_aug,
+    side_aug,
     col_aug,
-    cross_t,
+    cross,
     kernel_store,
     rs_send,
     rs_recv,
     ag,
     proj,
     work,
-    inner_buf,
     dirs,
+    acc,
+    side_recv,
+    img_send,
+    img_recv,
     curv_buf,
     chol_sem,
     rs_sems,
     ag_sems,
-    inner_sems,
     dir_sems,
     curv_sems,
+    img_sems,
+    side_sems,
     point_recv,
     point_fwd,
-    point_side,
-    point_back,
+    own_sems,
     share_sems,
 ):
     me = lax.axis_index("rows")
@@ -175,13 +179,24 @@
     others(lambda to: pl.semaphore_signal(
         barrier, inc=1, device_id={"rows": to}, device_id_type=pl.DeviceIdType.MESH))
 
-    right = row_of(pos + 1, 0)
+    upper = pos // half
+    partner = row_of(pos, 1)
     left = row_of(pos - 1, 0)
-    partner = row_of(pos, 1)
-    own_slot = points.at[me]
-    first_right = remote(points_ref, own_slot, point_fwd.at[me], point_recv.at[me], right)
-    first_left = remote(points_ref, own_slot, point_back, point_recv.at[me], left)
-    first_side = remote(points_ref, own_slot, point_side.at[me], point_recv.at[me], partner)
+    left_last = row_of(pos - 1, ((pos - 1 + chips) % chips) // half)
+    across = row_of(pos + half, upper)
+    taker = row_of(pos + half, 1 - upper)
+
+    def near(k):
+        return row_of(pos + k, 0)
+
+    def back(k):
+        return row_of(pos - k, 0)
+
+    def hop(k, src, owner, to):
+        return remote(src, points.at[owner], point_fwd.at[k], point_recv.at[owner], to)
+
+    own_left = hop(0, points_ref, me, left if half > 1 else left_last)
+    own_side = remote(points_ref, points.at[me], own_sems.at[0], point_recv.at[me], partner)
 
     own_aug[0:feat, :] = points_ref[...]
     own_aug[feat:, :] = norm_rows(points_ref[...], True)
@@ -195,11 +210,13 @@
 
     def project(i, carry):
         at = pl.multiple_of(i * CHUNK, CHUNK)
-        parts = [part.astype(jnp.bfloat16) for part in split(entries(own_aug, at, col_aug))]
+        store_split(cross, (pl.ds(at, CHUNK), slice(None)), entries(own_aug, at, col_aug))
+        parts = [cross[term, pl.ds(at, CHUNK), :] for term in range(3)]
         proj[...] += dot_split(residual_ref[:, pl.ds(at, CHUNK)], parts, dot_nn)
         return carry
 
     lax.fori_loop(0, local // CHUNK, project, 0)
+    own_square = to_row(jnp.sum(residual_ref[...] * residual_ref[...], axis=1, keepdims=True), TILE)
 
     pl.semaphore_wait(barrier, n - 1)
 
@@ -208,31 +225,22 @@
     rows_per = outs * tiles // n
     for piece in range(n):
         h, j = piece // tiles, piece % tiles
-        rs_send[piece] = proj[h * rows_per:(h + 1) * rows_per, j * TILE:(j + 1) * TILE]
+        rs_send[piece, 0:rows_per] = proj[h * rows_per:(h + 1) * rows_per, j * TILE:(j + 1) * TILE]
+        rs_send[piece, rows_per:rows_per + 1] = own_square
     send_all(lambda to: rs_send.at[to], rs_recv, rs_sems)
-    rs_recv[me] = rs_send[me]
-    first_right.start()
-    first_left.start()
-    first_side.start()
-
-    def landmark_rows(i, carry):
-        at = pl.multiple_of(i * CHUNK, CHUNK)
-        store_split(cross_t, (pl.ds(at, CHUNK), slice(None)), entries(col_aug, at, own_aug))
-        return carry
-
-    lax.fori_loop(0, land // CHUNK, landmark_rows, 0)
-
-    def make_block(owner, slot):
-        col_aug[0:feat, :] = points[owner]
-        col_aug[feat:, :] = norm_rows(points[owner], False)
-
+    rs_recv[me, 0:rows_per + 1] = rs_send[me, 0:rows_per + 1]
+    own_left.start()
+    own_side.start()
+
+    def make_left(owner_points):
+        col_aug[0:feat, :] = owner_points[...]
+        col_aug[feat:, :] = norm_rows(owner_points[...], False)
+
+    def make_block(slot, right_aug):
         for at in range(0, local, CHUNK):
-            kernel_store[slot, at:at + CHUNK, :] = entries(col_aug, at, own_aug).astype(jnp.bfloat16)
-
-    own_points = pltpu.make_async_copy(points_ref, own_slot, chol_sem)
+            kernel_store[slot, at:at + CHUNK, :] = entries(col_aug, at, right_aug).astype(jnp.bfloat16)
+
     chol_copy.wait()
-    own_points.start()
-    own_points.wait()
 
     row = lax.broadcasted_iota(jnp.int32, (TILE, TILE), 0)
     col = lax.broadcasted_iota(jnp.int32, (TILE, TILE), 1)
@@ -262,63 +270,64 @@
         inverse[first + b] = inverted[b]
 
     wait_all(lambda to: rs_send.at[to], rs_recv, rs_sems)
-    ag[me] = jnp.sum(rs_recv[...], axis=0)
+    gathered = jnp.sum(rs_recv[:, 0:rows_per + 1], axis=0)
+    ag[me] = gathered[0:rows_per]
+    square = to_column(gathered[rows_per:rows_per + 1])
     send_all(lambda to: ag.at[me], ag, ag_sems)
 
     shares = inverse.at[pl.ds(first, share)]
     shared = remote(shares, shares, share_sems.at[0], share_sems.at[1], partner)
     shared.start()
 
-    def pass_on(s, both):
-        near = row_of(pos - s, 0)
-        remote(points_ref, points.at[near], point_fwd.at[near], point_recv.at[near], right).wait_recv()
-        if both:
-            remote(points.at[near], points.at[near], point_fwd.at[near], point_recv.at[near], right).start()
-        remote(points.at[near], points.at[near], point_side.at[near], point_recv.at[near], partner).start()
-        if both:
-            far = row_of(pos + s, 0)
-            remote(points_ref, points.at[far], point_fwd.at[far], point_recv.at[far], left).wait_recv()
-            remote(points.at[far], points.at[far], point_side.at[far], point_recv.at[far], partner).start()
-
-            @pl.when(s < half - 1)
-            def _():
-                remote(points.at[far], points.at[far], point_fwd.at[far], point_recv.at[far], left).start()
-
-    def build_lanes(s, both):
-        def build(lane):
-            def one(way, carry):
-                owner = row_of(pos - s + 2 * s * way, lane)
-                if lane == 1:
-                    remote(points_ref, points.at[owner], point_side.at[owner], point_recv.at[owner], partner).wait_recv()
-                if keep:
-                    make_block(owner, owner)
-                return carry
-
-            lax.fori_loop(0, 2 if both else 1, one, 0)
-
-        build(0)
-        build(1)
-
-    pass_on(1, True)
-    build_lanes(1, True)
-    remote(points_ref, points.at[partner], point_side.at[partner], point_recv.at[partner], partner).wait_recv()
+    def pass_on(k):
+        owner = near(k)
+        to = left_last if k == half - 1 else left
+        hop(k, points.at[owner], owner, left).wait_recv()
+        hop(k, points.at[owner], owner, to).start()
+
+    def pass_on_any(k):
+        owner = near(k)
+        hop(k, points.at[owner], owner, left).wait_recv()
+
+        @pl.when(k < half - 1)
+        def _():
+            hop(k, points.at[owner], owner, left).start()
+
+        @pl.when(k == half - 1)
+        def _():
+            hop(k, points.at[owner], owner, left_last).start()
+
+    own_slot, side_slot, across_slot = 2 * half - 1, 2 * half, 2 * half - 2
+
+    if half > 1:
+        pass_on(1)
+    remote(points_ref, points.at[partner], own_sems.at[0], point_recv.at[partner], partner).wait_recv()
+    side_aug[0:feat, :] = points[partner]
+    side_aug[feat:, :] = norm_rows(points[partner], True)
+    if keep:
+        make_left(points_ref)
+        make_block(own_slot, own_aug)
 
     other = inverse.at[pl.ds(share - first, share)]
     remote(other, other, share_sems.at[0], share_sems.at[1], partner).wait_recv()
     for b in range(groups):
-        upper, lower = inverse[2 * b], inverse[2 * b + 1]
+        upper_block, lower_block = inverse[2 * b], inverse[2 * b + 1]
         at, end = b * GROUP, (b + 1) * GROUP
         off = chol[at + TILE:end, at:at + TILE]
-        change = dot_nn(dot_nn(lower, off, HIGH), upper, HIGH)
-        zero = jnp.zeros_like(upper)
+        change = dot_nn(dot_nn(lower_block, off, HIGH), upper_block, HIGH)
+        zero = jnp.zeros_like(upper_block)
         whole = jnp.concatenate(
-            [jnp.concatenate([upper, zero], axis=1), jnp.concatenate([-change, lower], axis=1)], axis=0
+            [jnp.concatenate([upper_block, zero], axis=1), jnp.concatenate([-change, lower_block], axis=1)], axis=0
         )
         store_split(inverse_parts, (b,), whole)
         if b > 0:
             store_split(chol_parts, (slice(at, end), slice(0, at)), chol[at:end, :at])
 
-    pass_on(2, True)
+    if keep:
+        make_left(points.at[partner])
+        make_block(side_slot, own_aug)
+    if half > 2:
+        pass_on(2)
     wait_all(lambda to: ag.at[me], ag, ag_sems)
     for piece in range(n):
         h, j = piece // tiles, piece % tiles
@@ -336,6 +345,7 @@
         pieces[b] = dot_split(pieces[b], inverse_of(b), dot_nt)
         for i in range(b + 1, groups):
             pieces[i] = pieces[i] - dot_split(pieces[b], block_parts(i, b), dot_nt)
+    halfway = jnp.concatenate(pieces, axis=1)
     for b in reversed(range(groups)):
         pieces[b] = dot_split(pieces[b], inverse_of(b), dot_nn)
         for j in reversed(range(b)):
@@ -343,84 +353,163 @@
     coeffs = jnp.concatenate(pieces, axis=1)
 
     ridge = ridge_ref[0]
+    inner = (square - jnp.sum(halfway * halfway, axis=1, keepdims=True)) / ridge
+    inner_out[...] = to_row(inner, TILE)[:, :outs]
     residual = residual_ref[...]
-    precond = (residual - dot_split(coeffs, [cross_t.at[term][...] for term in range(3)], dot_nn)) / ridge
-    inner_buf[me] = to_row(jnp.sum(precond * residual, axis=1, keepdims=True), TILE)
-    send_all(lambda to: inner_buf.at[me], inner_buf, inner_sems)
-
-    pass_on(3, True)
-    if keep:
-        make_block(partner, partner)
-    build_lanes(2, True)
-    wait_all(lambda to: inner_buf.at[me], inner_buf, inner_sems)
-    inner_row = jnp.sum(inner_buf[...], axis=0)
-    inner_out[...] = inner_row[:, :outs]
-    inner = to_column(inner_row)
+    precond = (residual - dot_split(coeffs, [cross.at[term][...] for term in range(3)], dot_nt)) / ridge
     direction_new = precond + (inner / to_column(rz_ref[...])) * direction_ref[...]
     direction_out[...] = direction_new
     dirs[me] = direction_new.astype(jnp.bfloat16)
-    send_all(lambda to: dirs.at[me], dirs, dir_sems)
+
+    def dir_to(to):
+        return remote(dirs.at[me], dirs.at[to], dir_sems.at[0, to], dir_sems.at[1, me], to)
+
+    def send_dir(to):
+        remote(dirs.at[me], dirs.at[me], dir_sems.at[0, to], dir_sems.at[1, me], to).start()
+
+    def wait_dir(src):
+        remote(dirs.at[me], dirs.at[src], dir_sems.at[0, src], dir_sems.at[1, src], src).wait_recv()
+
+    send_dir(taker)
+    lax.fori_loop(1, half, lambda k, carry: (send_dir(back(half - k)), carry)[1], 0)
+    send_dir(partner)
+
+    def wait_across():
+        hop(0, points.at[across], across, left).wait_recv()
+
+    def make_pair(k, slot):
+        make_left(points.at[near(k)])
+        make_block(slot, own_aug)
+        make_block(slot + 1, side_aug)
+
+    acc[...] = jnp.zeros_like(acc)
+
+    def forward(owner, slot, side):
+        acc[1] += dot_nn(dirs[owner], kernel_store[slot])
+        if side:
+            acc[2] += dot_nn(dirs[owner], kernel_store[slot + 1])
+
+    def image_to(k, owner):
+        return remote(img_send.at[k], img_recv.at[k], img_sems.at[0, k], img_sems.at[1, k], owner)
+
+    def backward(k, owner, slot, side):
+        total = dot_nt(dirs[me], kernel_store[slot])
+        if side:
+            total = total + dot_nt(dirs[partner], kernel_store[slot + 1])
+        img_send[k] = total
+        image_to(k, owner).start()
+
+    def at_own():
+        acc[0] += dot_nn(dirs[me], kernel_store[own_slot if keep else 0])
+
+    def at_side():
+        acc[0] += dot_nn(dirs[partner], kernel_store[side_slot if keep else 0])
 
     if keep:
-        make_block(me, me)
-    build_lanes(3, True)
-
-    def later(s, carry):
-        pass_on(s, True)
-        build_lanes(s, True)
-        return carry
-
-    lax.fori_loop(4, half, later, 0)
-    pass_on(half, False)
-    build_lanes(half, False)
-
-    def image_part(owner, slot):
-        if not keep:
-            make_block(owner, slot)
-        proj[...] += dot_nn(dirs[owner], kernel_store[slot])
-
-    proj[...] = jnp.zeros_like(proj)
-    image_part(me, me if keep else 0)
-
-    def gather_image(to):
-        remote(dirs.at[me], dirs.at[to], dir_sems.at[0, to], dir_sems.at[1, to], to).wait_recv()
-        image_part(to, to if keep else 0)
-
-    others(gather_image)
-
+        for k in range(3, half):
+            pass_on(k)
+
+        def build(k, carry):
+            make_pair(k, 2 * (k - 1))
+            return carry
+
+        lax.fori_loop(1, half, build, 0)
+        wait_across()
+        make_left(points.at[across])
+        make_block(across_slot, own_aug)
+
+        at_own()
+        wait_dir(partner)
+        at_side()
+
+        def ahead(k, carry):
+            wait_dir(near(k))
+            forward(near(k), 2 * (k - 1), True)
+            return carry
+
+        lax.fori_loop(1, half, ahead, 0)
+        wait_dir(across)
+        forward(across, across_slot, False)
+    else:
+        make_left(points_ref)
+        make_block(0, own_aug)
+        at_own()
+        make_left(points.at[partner])
+        make_block(0, own_aug)
+        wait_dir(partner)
+        at_side()
+
+        def both(k, carry):
+            @pl.when(k > 2)
+            def _():
+                pass_on_any(k)
+
+            make_pair(k, 0)
+            wait_dir(near(k))
+            forward(near(k), 0, True)
+            backward(k - 1, near(k), 0, True)
+            return carry
+
+        lax.fori_loop(1, half, both, 0)
+        wait_across()
+        make_left(points.at[across])
+        make_block(0, own_aug)
+        wait_dir(across)
+        forward(across, 0, False)
+        backward(half - 1, across, 0, False)
+
+    side_send = remote(acc.at[2], side_recv, side_sems.at[0], side_sems.at[1], partner)
+    side_send.start()
     direction_new = direction_out[...]
-    image = proj[...] + ridge * direction_new
-    image_out[...] = image
-    curv_buf[me] = to_row(jnp.sum(direction_new * image, axis=1, keepdims=True), TILE)
+    once = direction_new * (acc[0] + 2.0 * acc[1] + ridge * direction_new)
+    twice = once + 2.0 * dirs[partner].astype(jnp.float32) * acc[2]
+    curv_buf[me] = to_row(jnp.sum(twice, axis=1, keepdims=True), TILE)
     send_all(lambda to: curv_buf.at[me], curv_buf, curv_sems)
+
+    if keep:
+        backward(half - 1, across, across_slot, False)
+
+        def behind(i, carry):
+            k = half - i
+            backward(k - 1, near(k), 2 * (k - 1), True)
+            return carry
+
+        lax.fori_loop(1, half, behind, 0)
+
+    side_send.wait_recv()
+    image = acc[0] + acc[1] + ridge * direction_new + side_recv[...]
 
     drain(lambda to: rs_send.at[to], rs_recv, rs_sems)
     drain(lambda to: ag.at[me], ag, ag_sems)
-    drain(lambda to: inner_buf.at[me], inner_buf, inner_sems)
-    drain(lambda to: dirs.at[me], dirs, dir_sems)
     shared.wait_send()
-    first_right.wait_send()
-    first_left.wait_send()
-    first_side.wait_send()
-
-    def relay_drain(s, both):
-        near = row_of(pos - s, 0)
-        remote(points.at[near], points.at[near], point_side.at[near], point_recv.at[near], partner).wait_send()
-        if both:
-            remote(points.at[near], points.at[near], point_fwd.at[near], point_recv.at[near], right).wait_send()
-            far = row_of(pos + s, 0)
-            remote(points.at[far], points.at[far], point_side.at[far], point_recv.at[far], partner).wait_send()
-
-            @pl.when(s < half - 1)
-            def _():
-                remote(points.at[far], points.at[far], point_fwd.at[far], point_recv.at[far], left).wait_send()
-
-    lax.fori_loop(1, half, lambda s, carry: (relay_drain(s, True), carry)[1], 0)
-    relay_drain(half, False)
+    own_left.wait_send()
+    own_side.wait_send()
+
+    def relay_drain(k, carry):
+        hop(k, points.at[near(k)], near(k), left).wait_send()
+        return carry
+
+    lax.fori_loop(1, half, relay_drain, 0)
+
+    def dir_drain(k, carry):
+        dir_to(back(k)).wait_send()
+        return carry
+
+    lax.fori_loop(1, half, dir_drain, 0)
+    dir_to(taker).wait_send()
+    dir_to(partner).wait_send()
+
+    for k in range(half):
+        image_to(k, across).wait_recv()
+        image = image + img_recv[k]
+    image_out[...] = image
 
     wait_all(lambda to: curv_buf.at[me], curv_buf, curv_sems)
     alpha_out[...] = inner_out[...] / jnp.sum(curv_buf[...], axis=0)[:, :outs]
     drain(lambda to: curv_buf.at[me], curv_buf, curv_sems)
+    side_send.wait_send()
+    for k in range(half):
+        image_to(k, across).wait_send()
 
 
 def finish(
@@ -451,7 +540,9 @@
         land = landmarks.shape[1]
         outs = residual.shape[0]
         keep = n <= STORED_BLOCKS
+        half = n // 4
         piece = outs * land // (TILE * n)
+        padded = -(-(piece + 1) // 8) * 8
         f32, bf16 = jnp.float32, jnp.bfloat16
         vmem = pl.BlockSpec(memory_space=pltpu.VMEM)
         wide = jax.ShapeDtypeStruct((outs, own), f32)
@@ -478,26 +569,30 @@
                 pltpu.VMEM((n, feat, own), bf16),
                 pltpu.VMEM((feat + 16, own), bf16),
                 pltpu.VMEM((feat + 16, own), bf16),
-                pltpu.VMEM((3, land, own), bf16),
-                pltpu.VMEM((n if keep else 1, own, own), bf16),
-                pltpu.VMEM((n, piece, TILE), f32),
-                pltpu.VMEM((n, piece, TILE), f32),
+                pltpu.VMEM((feat + 16, own), bf16),
+                pltpu.VMEM((3, own, land), bf16),
+                pltpu.VMEM((2 * half + 1 if keep else 2, own, own), bf16),
+                pltpu.VMEM((n, padded, TILE), f32),
+                pltpu.VMEM((n, padded, TILE), f32),
                 pltpu.VMEM((n, piece, TILE), f32),
                 pltpu.VMEM((outs, land), f32),
                 pltpu.VMEM((outs, land), f32),
-                pltpu.VMEM((n, 1, TILE), f32),
                 pltpu.VMEM((n, outs, own), bf16),
+                pltpu.VMEM((3, outs, own), f32),
+                pltpu.VMEM((outs, own), f32),
+                pltpu.VMEM((half, outs, own), f32),
+                pltpu.VMEM((half, outs, own), f32),
                 pltpu.VMEM((n, 1, TILE), f32),
                 dma,
                 dma((2, n)),
                 dma((2, n)),
                 dma((2, n)),
                 dma((2, n)),
-                dma((2, n)),
+                dma((2, half)),
+                dma((2,)),
                 dma((n,)),
-                dma((n,)),
-                dma((n,)),
-                dma,
+                dma((half,)),
+                dma((2,)),
                 dma((2,)),
             ],
             compiler_params=pltpu.CompilerParams(

time: 48.3 us -> 44.7 us (0.925)
  Pallas kernels: 46.8 us -> 43.2 us
    pallas_call x1, Pallas kernels: 45.3 us -> 41.6 us  [local(): pl.pallas_call(functools.partial(kernel, n, keep), out_shape=(wide, wide,...]
where the time goes in v1:
time: 44.7 us; the launch traced here: 44.5 us
  Pallas kernels  43.2 us (97%)
  between operations  1.29 us (3%)
    pallas_call x1, Pallas kernels, local(): pl.pallas_call(functools.partial(kernel, n, keep), out_shape=(wide, wide,...  41.6 us
    pallas_call x1, Pallas kernels, local(): pl.pallas_call(finish, out_shape=(wide, wide, wide, thin), in_specs=[vmem...  1.54 us

profile of v1, /device:TPU:0, one launch (start us, length us, event | category | flops | bytes accessed | tf_op | source)
XLA Modules:
  0.0 44.5 jit_solution(9442785341244770282)
XLA Ops:
  1.3 41.6 %cg_step.1 = (f32[8,1024]{1,0:T(8,128)}, f32[8,1024]{1,0:T(8,128)}, f32[1,8]{1,0:T(1,128)}, f32[1,8]{1,0:T(1,128)}) custom-call(bf16[64,1024]{1,0:T(8,128)(2,1)} %points_ref.1, bf16[64,1024]{1,0:T(8,128)(2,1)} %landmarks_ref.1, f32[1024,1024]{1,0:T(8,128)} %chol_hbm.1, f32[1]{0:T(128)S(6)} %copy.12.ridge_ref, f32[8,1024]{1,0:T(8,128)} %residual_ref.3, ...), custom_call_target="tpu_custom_call" | custom-call | tf_op jit(solution)/shard_map/cg_step/pallas_call | solution.py:551
  42.9 1.5 %finish.1 = (f32[8,1024]{1,0:T(8,128)}, f32[8,1024]{1,0:T(8,128)}, f32[8,1024]{1,0:T(8,128)}, f32[1,8]{1,0:T(1,128)}) custom-call(f32[8,1024]{1,0:T(8,128)} %get-tuple-element.12.image_ref, f32[8,1024]{1,0:T(8,128)} %get-tuple-element.13.direction_ref, f32[1,8]{1,0:T(1,128)} %get-tuple-element.14.inner_ref, f32[1,8]{1,0:T(1,128)} %get-tuple-element.15.alpha_ref, ...), custom_call_target="tpu_custom_call" | custom-call | tf_op jit(solution)/shard_map/finish/pallas_call | solution.py:603

commit v2 on v1

--- a/solution.py
+++ b/solution.py
@@ -269,44 +269,43 @@
     for b in range(share):
         inverse[first + b] = inverted[b]
 
+    shares = inverse.at[pl.ds(first, share)]
+    shared = remote(shares, shares, share_sems.at[0], share_sems.at[1], partner)
+    shared.start()
+
+    def pass_on(k):
+        owner = near(k)
+        to = left_last if k == half - 1 else left
+        hop(k, points.at[owner], owner, left).wait_recv()
+        hop(k, points.at[owner], owner, to).start()
+
+    def pass_on_any(k):
+        owner = near(k)
+        hop(k, points.at[owner], owner, left).wait_recv()
+
+        @pl.when(k < half - 1)
+        def _():
+            hop(k, points.at[owner], owner, left).start()
+
+        @pl.when(k == half - 1)
+        def _():
+            hop(k, points.at[owner], owner, left_last).start()
+
+    own_slot, side_slot, across_slot = 2 * half - 1, 2 * half, 2 * half - 2
+
+    if keep:
+        make_left(points_ref)
+        make_block(own_slot, own_aug)
+    remote(points_ref, points.at[partner], own_sems.at[0], point_recv.at[partner], partner).wait_recv()
+    side_aug[0:feat, :] = points[partner]
+    side_aug[feat:, :] = norm_rows(points[partner], True)
     wait_all(lambda to: rs_send.at[to], rs_recv, rs_sems)
     gathered = jnp.sum(rs_recv[:, 0:rows_per + 1], axis=0)
     ag[me] = gathered[0:rows_per]
     square = to_column(gathered[rows_per:rows_per + 1])
     send_all(lambda to: ag.at[me], ag, ag_sems)
-
-    shares = inverse.at[pl.ds(first, share)]
-    shared = remote(shares, shares, share_sems.at[0], share_sems.at[1], partner)
-    shared.start()
-
-    def pass_on(k):
-        owner = near(k)
-        to = left_last if k == half - 1 else left
-        hop(k, points.at[owner], owner, left).wait_recv()
-        hop(k, points.at[owner], owner, to).start()
-
-    def pass_on_any(k):
-        owner = near(k)
-        hop(k, points.at[owner], owner, left).wait_recv()
-
-        @pl.when(k < half - 1)
-        def _():
-            hop(k, points.at[owner], owner, left).start()
-
-        @pl.when(k == half - 1)
-        def _():
-            hop(k, points.at[owner], owner, left_last).start()
-
-    own_slot, side_slot, across_slot = 2 * half - 1, 2 * half, 2 * half - 2
-
     if half > 1:
         pass_on(1)
-    remote(points_ref, points.at[partner], own_sems.at[0], point_recv.at[partner], partner).wait_recv()
-    side_aug[0:feat, :] = points[partner]
-    side_aug[feat:, :] = norm_rows(points[partner], True)
-    if keep:
-        make_left(points_ref)
-        make_block(own_slot, own_aug)
 
     other = inverse.at[pl.ds(share - first, share)]
     remote(other, other, share_sems.at[0], share_sems.at[1], partner).wait_recv()
@@ -323,11 +322,16 @@
         if b > 0:
             store_split(chol_parts, (slice(at, end), slice(0, at)), chol[at:end, :at])
 
+    def make_pair(k, slot):
+        make_left(points.at[near(k)])
+        make_block(slot, own_aug)
+        make_block(slot + 1, side_aug)
+
     if keep:
         make_left(points.at[partner])
         make_block(side_slot, own_aug)
-    if half > 2:
-        pass_on(2)
+        if half > 1:
+            make_pair(1, 0)
     wait_all(lambda to: ag.at[me], ag, ag_sems)
     for piece in range(n):
         h, j = piece // tiles, piece % tiles
@@ -346,6 +350,8 @@
         for i in range(b + 1, groups):
             pieces[i] = pieces[i] - dot_split(pieces[b], block_parts(i, b), dot_nt)
     halfway = jnp.concatenate(pieces, axis=1)
+    if half > 2:
+        pass_on(2)
     for b in reversed(range(groups)):
         pieces[b] = dot_split(pieces[b], inverse_of(b), dot_nn)
         for j in reversed(range(b)):
@@ -373,14 +379,11 @@
     send_dir(taker)
     lax.fori_loop(1, half, lambda k, carry: (send_dir(back(half - k)), carry)[1], 0)
     send_dir(partner)
+    if keep and half > 3:
+        pass_on(3)
 
     def wait_across():
         hop(0, points.at[across], across, left).wait_recv()
-
-    def make_pair(k, slot):
-        make_left(points.at[near(k)])
-        make_block(slot, own_aug)
-        make_block(slot + 1, side_aug)
 
     acc[...] = jnp.zeros_like(acc)
 
@@ -398,46 +401,41 @@
             total = total + dot_nt(dirs[partner], kernel_store[slot + 1])
         img_send[k] = total
         image_to(k, owner).start()
-
-    def at_own():
-        acc[0] += dot_nn(dirs[me], kernel_store[own_slot if keep else 0])
-
-    def at_side():
-        acc[0] += dot_nn(dirs[partner], kernel_store[side_slot if keep else 0])
+        wait_dir(owner)
+        acc[3] += total * dirs[owner].astype(jnp.float32)
+
+    def at_own(slot):
+        acc[0] += dot_nn(dirs[me], kernel_store[slot])
+
+    def at_side(slot):
+        acc[0] += dot_nn(dirs[partner], kernel_store[slot])
 
     if keep:
-        for k in range(3, half):
-            pass_on(k)
-
-        def build(k, carry):
+        for k in range(2, half):
+            if k > 3:
+                pass_on(k)
             make_pair(k, 2 * (k - 1))
-            return carry
-
-        lax.fori_loop(1, half, build, 0)
+            if k == 2:
+                wait_dir(partner)
+            backward(k - 1, near(k), 2 * (k - 1), True)
+        if half < 3:
+            wait_dir(partner)
         wait_across()
         make_left(points.at[across])
         make_block(across_slot, own_aug)
-
-        at_own()
-        wait_dir(partner)
-        at_side()
-
-        def ahead(k, carry):
-            wait_dir(near(k))
-            forward(near(k), 2 * (k - 1), True)
-            return carry
-
-        lax.fori_loop(1, half, ahead, 0)
-        wait_dir(across)
-        forward(across, across_slot, False)
+        backward(half - 1, across, across_slot, False)
+        if half > 1:
+            backward(0, near(1), 0, True)
+        at_own(own_slot)
+        at_side(side_slot)
     else:
         make_left(points_ref)
         make_block(0, own_aug)
-        at_own()
+        at_own(0)
         make_left(points.at[partner])
         make_block(0, own_aug)
         wait_dir(partner)
-        at_side()
+        at_side(0)
 
         def both(k, carry):
             @pl.when(k > 2)
@@ -445,39 +443,34 @@
                 pass_on_any(k)
 
             make_pair(k, 0)
-            wait_dir(near(k))
+            backward(k - 1, near(k), 0, True)
             forward(near(k), 0, True)
-            backward(k - 1, near(k), 0, True)
             return carry
 
         lax.fori_loop(1, half, both, 0)
         wait_across()
         make_left(points.at[across])
         make_block(0, own_aug)
-        wait_dir(across)
+        backward(half - 1, across, 0, False)
         forward(across, 0, False)
-        backward(half - 1, across, 0, False)
+
+    direction_new = direction_out[...]
+    own_terms = direction_new * (acc[0] + ridge * direction_new) + 2.0 * acc[3]
+    curv_buf[me] = to_row(jnp.sum(own_terms, axis=1, keepdims=True), TILE)
+    send_all(lambda to: curv_buf.at[me], curv_buf, curv_sems)
+
+    if keep:
+        def ahead(k, carry):
+            forward(near(k), 2 * (k - 1), True)
+            return carry
+
+        lax.fori_loop(1, half, ahead, 0)
 
     side_send = remote(acc.at[2], side_recv, side_sems.at[0], side_sems.at[1], partner)
     side_send.start()
-    direction_new = direction_out[...]
-    once = direction_new * (acc[0] + 2.0 * acc[1] + ridge * direction_new)
-    twice = once + 2.0 * dirs[partner].astype(jnp.float32) * acc[2]
-    curv_buf[me] = to_row(jnp.sum(twice, axis=1, keepdims=True), TILE)
-    send_all(lambda to: curv_buf.at[me], curv_buf, curv_sems)
 
     if keep:
-        backward(half - 1, across, across_slot, False)
-
-        def behind(i, carry):
-            k = half - i
-            backward(k - 1, near(k), 2 * (k - 1), True)
-            return carry
-
-        lax.fori_loop(1, half, behind, 0)
-
-    side_send.wait_recv()
-    image = acc[0] + acc[1] + ridge * direction_new + side_recv[...]
+        forward(across, across_slot, False)
 
     drain(lambda to: rs_send.at[to], rs_recv, rs_sems)
     drain(lambda to: ag.at[me], ag, ag_sems)
@@ -499,6 +492,8 @@
     dir_to(taker).wait_send()
     dir_to(partner).wait_send()
 
+    side_send.wait_recv()
+    image = acc[0] + acc[1] + ridge * direction_new + side_recv[...]
     for k in range(half):
         image_to(k, across).wait_recv()
         image = image + img_recv[k]
@@ -578,7 +573,7 @@
                 pltpu.VMEM((outs, land), f32),
                 pltpu.VMEM((outs, land), f32),
                 pltpu.VMEM((n, outs, own), bf16),
-                pltpu.VMEM((3, outs, own), f32),
+                pltpu.VMEM((4, outs, own), f32),
                 pltpu.VMEM((outs, own), f32),
                 pltpu.VMEM((half, outs, own), f32),
                 pltpu.VMEM((half, outs, own), f32),

time: 44.7 us -> 39.8 us (0.89)
  Pallas kernels: 43.2 us -> 38.3 us
    pallas_call x1, Pallas kernels: 41.6 us -> 36.8 us  [local(): pl.pallas_call(functools.partial(kernel, n, keep), out_shape=(wide, wide,...]
where the time goes in v2:
time: 39.8 us; the launch traced here: 39.6 us
  Pallas kernels  38.3 us (96%)
  between operations  1.29 us (3%)
    pallas_call x1, Pallas kernels, local(): pl.pallas_call(functools.partial(kernel, n, keep), out_shape=(wide, wide,...  36.8 us
    pallas_call x1, Pallas kernels, local(): pl.pallas_call(finish, out_shape=(wide, wide, wide, thin), in_specs=[vmem...  1.54 us

profile of v2, /device:TPU:0, one launch (start us, length us, event | category | flops | bytes accessed | tf_op | source)
XLA Modules:
  0.0 39.6 jit_solution(5219462516754642207)
XLA Ops:
  1.3 36.8 %cg_step.1 = (f32[8,1024]{1,0:T(8,128)}, f32[8,1024]{1,0:T(8,128)}, f32[1,8]{1,0:T(1,128)}, f32[1,8]{1,0:T(1,128)}) custom-call(bf16[64,1024]{1,0:T(8,128)(2,1)} %points_ref.1, bf16[64,1024]{1,0:T(8,128)(2,1)} %landmarks_ref.1, f32[1024,1024]{1,0:T(8,128)} %chol_hbm.1, f32[1]{0:T(128)S(6)} %copy.12.ridge_ref, f32[8,1024]{1,0:T(8,128)} %residual_ref.3, ...), custom_call_target="tpu_custom_call" | custom-call | tf_op jit(solution)/shard_map/cg_step/pallas_call | solution.py:546
  38.1 1.5 %finish.1 = (f32[8,1024]{1,0:T(8,128)}, f32[8,1024]{1,0:T(8,128)}, f32[8,1024]{1,0:T(8,128)}, f32[1,8]{1,0:T(1,128)}) custom-call(f32[8,1024]{1,0:T(8,128)} %get-tuple-element.12.image_ref, f32[8,1024]{1,0:T(8,128)} %get-tuple-element.13.direction_ref, f32[1,8]{1,0:T(1,128)} %get-tuple-element.14.inner_ref, f32[1,8]{1,0:T(1,128)} %get-tuple-element.15.alpha_ref, ...), custom_call_target="tpu_custom_call" | custom-call | tf_op jit(solution)/shard_map/finish/pallas_call | solution.py:598

commit v3 on v2

--- a/solution.py
+++ b/solution.py
@@ -53,6 +53,14 @@
     low = dot(stacked[:2 * outs], parts[2])
     small = low[:outs] + mid[outs:] + high[2 * outs:]
     return high[:outs] + (high[outs:2 * outs] + mid[:outs] + small)
+
+
+def dot_pair(left, parts, dot):
+    outs = left.shape[0]
+    top = left.astype(jnp.bfloat16)
+    rest = (left - top.astype(jnp.float32)).astype(jnp.bfloat16)
+    high = dot(jnp.concatenate([top, rest], axis=0), parts[0])
+    return high[:outs] + (high[outs:] + dot(top, parts[1]))
 
 
 def norm_rows(features, first):
@@ -210,9 +218,12 @@
 
     def project(i, carry):
         at = pl.multiple_of(i * CHUNK, CHUNK)
-        store_split(cross, (pl.ds(at, CHUNK), slice(None)), entries(own_aug, at, col_aug))
-        parts = [cross[term, pl.ds(at, CHUNK), :] for term in range(3)]
-        proj[...] += dot_split(residual_ref[:, pl.ds(at, CHUNK)], parts, dot_nn)
+        values = entries(own_aug, at, col_aug)
+        top = values.astype(jnp.bfloat16)
+        cross[0, pl.ds(at, CHUNK), :] = top
+        cross[1, pl.ds(at, CHUNK), :] = (values - top.astype(jnp.float32)).astype(jnp.bfloat16)
+        parts = [cross[term, pl.ds(at, CHUNK), :] for term in range(2)]
+        proj[...] += dot_pair(residual_ref[:, pl.ds(at, CHUNK)], parts, dot_nn)
         return carry
 
     lax.fori_loop(0, local // CHUNK, project, 0)
@@ -358,11 +369,11 @@
             pieces[j] = pieces[j] - dot_split(pieces[b], block_parts(b, j), dot_nn)
     coeffs = jnp.concatenate(pieces, axis=1)
 
-    ridge = ridge_ref[0]
+    ridge = ridge_ref[...]
     inner = (square - jnp.sum(halfway * halfway, axis=1, keepdims=True)) / ridge
     inner_out[...] = to_row(inner, TILE)[:, :outs]
     residual = residual_ref[...]
-    precond = (residual - dot_split(coeffs, [cross.at[term][...] for term in range(3)], dot_nt)) / ridge
+    precond = (residual - dot_pair(coeffs, [cross.at[term][...] for term in range(2)], dot_nt)) / ridge
     direction_new = precond + (inner / to_column(rz_ref[...])) * direction_ref[...]
     direction_out[...] = direction_new
     dirs[me] = direction_new.astype(jnp.bfloat16)
@@ -401,14 +412,18 @@
             total = total + dot_nt(dirs[partner], kernel_store[slot + 1])
         img_send[k] = total
         image_to(k, owner).start()
-        wait_dir(owner)
-        acc[3] += total * dirs[owner].astype(jnp.float32)
+        return total
 
     def at_own(slot):
         acc[0] += dot_nn(dirs[me], kernel_store[slot])
 
     def at_side(slot):
         acc[0] += dot_nn(dirs[partner], kernel_store[slot])
+
+    early = 3
+
+    def terms_behind(total, owner):
+        acc[3] += total * dirs[owner].astype(jnp.float32)
 
     if keep:
         for k in range(2, half):
@@ -417,17 +432,29 @@
             make_pair(k, 2 * (k - 1))
             if k == 2:
                 wait_dir(partner)
-            backward(k - 1, near(k), 2 * (k - 1), True)
+            if k >= early:
+                sent = backward(k - 1, near(k), 2 * (k - 1), True)
+                wait_dir(near(k))
+                terms_behind(sent, near(k))
         if half < 3:
             wait_dir(partner)
         wait_across()
         make_left(points.at[across])
         make_block(across_slot, own_aug)
-        backward(half - 1, across, across_slot, False)
-        if half > 1:
-            backward(0, near(1), 0, True)
+        sent = backward(half - 1, across, across_slot, False)
         at_own(own_slot)
         at_side(side_slot)
+        wait_dir(across)
+        terms_behind(sent, across)
+
+        def ahead(k, carry):
+            wait_dir(near(k))
+            forward(near(k), 2 * (k - 1), True)
+            return carry
+
+        lax.fori_loop(1, min(half, early), ahead, 0)
+        low = dirs[partner].astype(jnp.float32)
+        acc[3] += direction_out[...] * acc[1] + low * acc[2]
     else:
         make_left(points_ref)
         make_block(0, own_aug)
@@ -444,6 +471,7 @@
 
             make_pair(k, 0)
             backward(k - 1, near(k), 0, True)
+            wait_dir(near(k))
             forward(near(k), 0, True)
             return carry
 
@@ -452,7 +480,10 @@
         make_left(points.at[across])
         make_block(0, own_aug)
         backward(half - 1, across, 0, False)
+        wait_dir(across)
         forward(across, 0, False)
+        low = dirs[partner].astype(jnp.float32)
+        acc[3] = direction_out[...] * acc[1] + low * acc[2]
 
     direction_new = direction_out[...]
     own_terms = direction_new * (acc[0] + ridge * direction_new) + 2.0 * acc[3]
@@ -460,11 +491,16 @@
     send_all(lambda to: curv_buf.at[me], curv_buf, curv_sems)
 
     if keep:
-        def ahead(k, carry):
+        last = min(half, early)
+
+        def behind(i, carry):
+            k = last - i
+            backward(k - 1, near(k), 2 * (k - 1), True)
+            return carry
+
+        lax.fori_loop(1, last, behind, 0)
+        for k in range(early, half):
             forward(near(k), 2 * (k - 1), True)
-            return carry
-
-        lax.fori_loop(1, half, ahead, 0)
 
     side_send = remote(acc.at[2], side_recv, side_sems.at[0], side_sems.at[1], partner)
     side_send.start()
@@ -550,7 +586,7 @@
                 vmem,
                 vmem,
                 pl.BlockSpec(memory_space=pl.ANY),
-                pl.BlockSpec(memory_space=pltpu.SMEM),
+                vmem,
                 vmem,
                 vmem,
                 vmem,
@@ -565,7 +601,7 @@
                 pltpu.VMEM((feat + 16, own), bf16),
                 pltpu.VMEM((feat + 16, own), bf16),
                 pltpu.VMEM((feat + 16, own), bf16),
-                pltpu.VMEM((3, own, land), bf16),
+                pltpu.VMEM((2, own, land), bf16),
                 pltpu.VMEM((2 * half + 1 if keep else 2, own, own), bf16),
                 pltpu.VMEM((n, padded, TILE), f32),
                 pltpu.VMEM((n, padded, TILE), f32),
@@ -594,7 +630,7 @@
                 collective_id=0, has_side_effects=True, vmem_limit_bytes=62 * 1024 * 1024
             ),
             name="cg_step",
-        )(points, landmarks, chol, ridge, residual, direction, rz_prev.reshape(1, outs))
+        )(points, landmarks, chol, ridge.reshape(1, 1), residual, direction, rz_prev.reshape(1, outs))
         results = pl.pallas_call(
             finish,
             out_shape=(wide, wide, wide, thin),

time: 39.8 us -> 40.5 us (1.018)
  Pallas kernels: 38.3 us -> 39 us
    pallas_call x1, Pallas kernels: 36.8 us -> 37.5 us  [local(): pl.pallas_call(functools.partial(kernel, n, keep), out_shape=(wide, wide,...]
where the time goes in v3:
time: 40.5 us; the launch traced here: 40.3 us
  Pallas kernels  39 us (96%)
  between operations  1.29 us (3%)
    pallas_call x1, Pallas kernels, local(): pl.pallas_call(functools.partial(kernel, n, keep), out_shape=(wide, wide,...  37.5 us
    pallas_call x1, Pallas kernels, local(): pl.pallas_call(finish, out_shape=(wide, wide, wide, thin), in_specs=[vmem...  1.54 us

profile of v3, /device:TPU:0, one launch (start us, length us, event | category | flops | bytes accessed | tf_op | source)
XLA Modules:
  0.0 40.3 jit_solution(16515949735614612957)
XLA Ops:
  1.3 37.5 %cg_step.1 = (f32[8,1024]{1,0:T(8,128)}, f32[8,1024]{1,0:T(8,128)}, f32[1,8]{1,0:T(1,128)}, f32[1,8]{1,0:T(1,128)}) custom-call(bf16[64,1024]{1,0:T(8,128)(2,1)} %points_ref.1, bf16[64,1024]{1,0:T(8,128)(2,1)} %landmarks_ref.1, f32[1024,1024]{1,0:T(8,128)} %chol_hbm.1, f32[1,1]{1,0:T(1,128)} %bitcast.3.ridge_ref, f32[8,1024]{1,0:T(8,128)} %residual_ref.3, ...), custom_call_target="tpu_custom_call" | custom-call | tf_op jit(solution)/shard_map/cg_step/pallas_call | solution.py:582
  38.8 1.5 %finish.1 = (f32[8,1024]{1,0:T(8,128)}, f32[8,1024]{1,0:T(8,128)}, f32[8,1024]{1,0:T(8,128)}, f32[1,8]{1,0:T(1,128)}) custom-call(f32[8,1024]{1,0:T(8,128)} %get-tuple-element.12.image_ref, f32[8,1024]{1,0:T(8,128)} %get-tuple-element.13.direction_ref, f32[1,8]{1,0:T(1,128)} %get-tuple-element.14.inner_ref, f32[1,8]{1,0:T(1,128)} %get-tuple-element.15.alpha_ref, ...), custom_call_target="tpu_custom_call" | custom-call | tf_op jit(solution)/shard_map/finish/pallas_call | solution.py:634

commit v4 on v3

--- a/solution.py
+++ b/solution.py
@@ -200,11 +200,12 @@
     def back(k):
         return row_of(pos - k, 0)
 
-    def hop(k, src, owner, to):
-        return remote(src, points.at[owner], point_fwd.at[k], point_recv.at[owner], to)
-
-    own_left = hop(0, points_ref, me, left if half > 1 else left_last)
-    own_side = remote(points_ref, points.at[me], own_sems.at[0], point_recv.at[me], partner)
+    def hop(k, h, src, owner, to):
+        part = pl.ds(h * (feat // 2), feat // 2)
+        return remote(src.at[part], points.at[owner, part], point_fwd.at[k, h], point_recv.at[owner, h], to)
+
+    own_left = [hop(0, h, points_ref, me, left if half > 1 else left_last) for h in range(2)]
+    own_side = remote(points_ref, points.at[me], own_sems.at[0], own_sems.at[1], partner)
 
     own_aug[0:feat, :] = points_ref[...]
     own_aug[feat:, :] = norm_rows(points_ref[...], True)
@@ -240,8 +241,9 @@
         rs_send[piece, rows_per:rows_per + 1] = own_square
     send_all(lambda to: rs_send.at[to], rs_recv, rs_sems)
     rs_recv[me, 0:rows_per + 1] = rs_send[me, 0:rows_per + 1]
-    own_left.start()
     own_side.start()
+    for copy in own_left:
+        copy.start()
 
     def make_left(owner_points):
         col_aug[0:feat, :] = owner_points[...]
@@ -284,30 +286,33 @@
     shared = remote(shares, shares, share_sems.at[0], share_sems.at[1], partner)
     shared.start()
 
-    def pass_on(k):
+    def pass_on(k, h):
         owner = near(k)
         to = left_last if k == half - 1 else left
-        hop(k, points.at[owner], owner, left).wait_recv()
-        hop(k, points.at[owner], owner, to).start()
+        hop(k, h, points.at[owner], owner, left).wait_recv()
+        hop(k, h, points.at[owner], owner, to).start()
 
     def pass_on_any(k):
         owner = near(k)
-        hop(k, points.at[owner], owner, left).wait_recv()
+        for h in range(2):
+            hop(k, h, points.at[owner], owner, left).wait_recv()
 
         @pl.when(k < half - 1)
         def _():
-            hop(k, points.at[owner], owner, left).start()
+            for h in range(2):
+                hop(k, h, points.at[owner], owner, left).start()
 
         @pl.when(k == half - 1)
         def _():
-            hop(k, points.at[owner], owner, left_last).start()
+            for h in range(2):
+                hop(k, h, points.at[owner], owner, left_last).start()
 
     own_slot, side_slot, across_slot = 2 * half - 1, 2 * half, 2 * half - 2
 
     if keep:
         make_left(points_ref)
         make_block(own_slot, own_aug)
-    remote(points_ref, points.at[partner], own_sems.at[0], point_recv.at[partner], partner).wait_recv()
+    remote(points_ref, points.at[partner], own_sems.at[0], own_sems.at[1], partner).wait_recv()
     side_aug[0:feat, :] = points[partner]
     side_aug[feat:, :] = norm_rows(points[partner], True)
     wait_all(lambda to: rs_send.at[to], rs_recv, rs_sems)
@@ -316,7 +321,7 @@
     square = to_column(gathered[rows_per:rows_per + 1])
     send_all(lambda to: ag.at[me], ag, ag_sems)
     if half > 1:
-        pass_on(1)
+        pass_on(1, 0)
 
     other = inverse.at[pl.ds(share - first, share)]
     remote(other, other, share_sems.at[0], share_sems.at[1], partner).wait_recv()
@@ -338,11 +343,15 @@
         make_block(slot, own_aug)
         make_block(slot + 1, side_aug)
 
+    if half > 1:
+        pass_on(1, 1)
     if keep:
         make_left(points.at[partner])
         make_block(side_slot, own_aug)
         if half > 1:
             make_pair(1, 0)
+    if half > 2:
+        pass_on(2, 0)
     wait_all(lambda to: ag.at[me], ag, ag_sems)
     for piece in range(n):
         h, j = piece // tiles, piece % tiles
@@ -362,7 +371,7 @@
             pieces[i] = pieces[i] - dot_split(pieces[b], block_parts(i, b), dot_nt)
     halfway = jnp.concatenate(pieces, axis=1)
     if half > 2:
-        pass_on(2)
+        pass_on(2, 1)
     for b in reversed(range(groups)):
         pieces[b] = dot_split(pieces[b], inverse_of(b), dot_nn)
         for j in reversed(range(b)):
@@ -391,10 +400,11 @@
     lax.fori_loop(1, half, lambda k, carry: (send_dir(back(half - k)), carry)[1], 0)
     send_dir(partner)
     if keep and half > 3:
-        pass_on(3)
+        pass_on(3, 0)
 
     def wait_across():
-        hop(0, points.at[across], across, left).wait_recv()
+        for h in range(2):
+            hop(0, h, points.at[across], across, left).wait_recv()
 
     acc[...] = jnp.zeros_like(acc)
 
@@ -428,8 +438,11 @@
     if keep:
         for k in range(2, half):
             if k > 3:
-                pass_on(k)
+                pass_on(k, 0)
+                pass_on(k, 1)
             make_pair(k, 2 * (k - 1))
+            if k == 2 and half > 3:
+                pass_on(3, 1)
             if k == 2:
                 wait_dir(partner)
             if k >= early:
@@ -438,23 +451,23 @@
                 terms_behind(sent, near(k))
         if half < 3:
             wait_dir(partner)
+        at_own(own_slot)
+        at_side(side_slot)
+
+        def ahead(k, carry):
+            wait_dir(near(k))
+            forward(near(k), 2 * (k - 1), True)
+            return carry
+
+        lax.fori_loop(1, min(half, early), ahead, 0)
+        low = dirs[partner].astype(jnp.float32)
+        acc[3] += direction_out[...] * acc[1] + low * acc[2]
         wait_across()
         make_left(points.at[across])
         make_block(across_slot, own_aug)
         sent = backward(half - 1, across, across_slot, False)
-        at_own(own_slot)
-        at_side(side_slot)
         wait_dir(across)
         terms_behind(sent, across)
-
-        def ahead(k, carry):
-            wait_dir(near(k))
-            forward(near(k), 2 * (k - 1), True)
-            return carry
-
-        lax.fori_loop(1, min(half, early), ahead, 0)
-        low = dirs[partner].astype(jnp.float32)
-        acc[3] += direction_out[...] * acc[1] + low * acc[2]
     else:
         make_left(points_ref)
         make_block(0, own_aug)
@@ -511,11 +524,13 @@
     drain(lambda to: rs_send.at[to], rs_recv, rs_sems)
     drain(lambda to: ag.at[me], ag, ag_sems)
     shared.wait_send()
-    own_left.wait_send()
+    for copy in own_left:
+        copy.wait_send()
     own_side.wait_send()
 
     def relay_drain(k, carry):
-        hop(k, points.at[near(k)], near(k), left).wait_send()
+        for h in range(2):
+            hop(k, h, points.at[near(k)], near(k), left).wait_send()
         return carry
 
     lax.fori_loop(1, half, relay_drain, 0)
@@ -621,8 +636,8 @@
                 dma((2, n)),
                 dma((2, half)),
                 dma((2,)),
-                dma((n,)),
-                dma((half,)),
+                dma((n, 2)),
+                dma((half, 2)),
                 dma((2,)),
                 dma((2,)),
             ],

time: 40.5 us -> 38.9 us (0.960)
  Pallas kernels: 39 us -> 37.4 us
    pallas_call x1, Pallas kernels: 37.5 us -> 35.8 us  [local(): pl.pallas_call(functools.partial(kernel, n, keep), out_shape=(wide, wide,...]
where the time goes in v4:
time: 38.9 us; the launch traced here: 38.6 us
  Pallas kernels  37.4 us (96%)
  between operations  1.29 us (3%)
    pallas_call x1, Pallas kernels, local(): pl.pallas_call(functools.partial(kernel, n, keep), out_shape=(wide, wide,...  35.8 us
    pallas_call x1, Pallas kernels, local(): pl.pallas_call(finish, out_shape=(wide, wide, wide, thin), in_specs=[vmem...  1.54 us

profile of v4, /device:TPU:0, one launch (start us, length us, event | category | flops | bytes accessed | tf_op | source)
XLA Modules:
  0.0 38.6 jit_solution(15942304625454407874)
XLA Ops:
  1.3 35.8 %cg_step.1 = (f32[8,1024]{1,0:T(8,128)}, f32[8,1024]{1,0:T(8,128)}, f32[1,8]{1,0:T(1,128)}, f32[1,8]{1,0:T(1,128)}) custom-call(bf16[64,1024]{1,0:T(8,128)(2,1)} %points_ref.1, bf16[64,1024]{1,0:T(8,128)(2,1)} %landmarks_ref.1, f32[1024,1024]{1,0:T(8,128)} %chol_hbm.1, f32[1,1]{1,0:T(1,128)} %bitcast.3.ridge_ref, f32[8,1024]{1,0:T(8,128)} %residual_ref.3, ...), custom_call_target="tpu_custom_call" | custom-call | tf_op jit(solution)/shard_map/cg_step/pallas_call | solution.py:597
  37.1 1.5 %finish.1 = (f32[8,1024]{1,0:T(8,128)}, f32[8,1024]{1,0:T(8,128)}, f32[8,1024]{1,0:T(8,128)}, f32[1,8]{1,0:T(1,128)}) custom-call(f32[8,1024]{1,0:T(8,128)} %get-tuple-element.12.image_ref, f32[8,1024]{1,0:T(8,128)} %get-tuple-element.13.direction_ref, f32[1,8]{1,0:T(1,128)} %get-tuple-element.14.inner_ref, f32[1,8]{1,0:T(1,128)} %get-tuple-element.15.alpha_ref, ...), custom_call_target="tpu_custom_call" | custom-call | tf_op jit(solution)/shard_map/finish/pallas_call | solution.py:649

commit v5 on v4

--- a/solution.py
+++ b/solution.py
@@ -8,22 +8,22 @@
 from jax.experimental.pallas import tpu as pltpu
 from jax.sharding import PartitionSpec as P
 
-HIGH = lax.Precision.HIGHEST
 TILE = 128
 CHUNK = 256
 GROUP = 2 * TILE
 STORED_BLOCKS = 16
-
-
-def dot_nn(left, right, precision=None):
+LIMIT = 62
+
+
+def dot_nn(left, right):
     return lax.dot_general(
-        left, right, (((1,), (0,)), ((), ())), precision=precision, preferred_element_type=jnp.float32
+        left, right, (((1,), (0,)), ((), ())), preferred_element_type=jnp.float32
     )
 
 
-def dot_nt(left, right, precision=None):
+def dot_nt(left, right):
     return lax.dot_general(
-        left, right, (((1,), (1,)), ((), ())), precision=precision, preferred_element_type=jnp.float32
+        left, right, (((1,), (1,)), ((), ())), preferred_element_type=jnp.float32
     )
 
 
@@ -33,32 +33,28 @@
     )
 
 
-def split(values):
-    top = values.astype(jnp.bfloat16).astype(jnp.float32)
-    rest = values - top
-    mid = rest.astype(jnp.bfloat16).astype(jnp.float32)
-    return top, mid, rest - mid
-
-
-def store_split(ref, at, values):
-    for term, part in enumerate(split(values)):
-        ref[(term,) + at] = part.astype(jnp.bfloat16)
-
-
-def dot_split(left, parts, dot):
-    outs = left.shape[0]
-    stacked = jnp.concatenate(split(left), axis=0).astype(jnp.bfloat16)
-    high = dot(stacked, parts[0])
-    mid = dot(stacked[:2 * outs], parts[1])
-    low = dot(stacked[:2 * outs], parts[2])
-    small = low[:outs] + mid[outs:] + high[2 * outs:]
-    return high[:outs] + (high[outs:2 * outs] + mid[:outs] + small)
+def halves(values):
+    top = values.astype(jnp.bfloat16)
+    return top, (values - top.astype(jnp.float32)).astype(jnp.bfloat16)
+
+
+def dot_square(left, right):
+    width = right.shape[1]
+    first, second = halves(right)
+    upper = jnp.concatenate([first, second], axis=1)
+    lower = jnp.concatenate([jnp.zeros_like(first), first], axis=1)
+    both = dot_nn(jnp.concatenate(halves(left), axis=1), jnp.concatenate([upper, lower], axis=0))
+    return both[:, :width] + both[:, width:]
+
+
+def store_pair(ref, at, values):
+    for term, part in enumerate(halves(values)):
+        ref[(term,) + at] = part
 
 
 def dot_pair(left, parts, dot):
     outs = left.shape[0]
-    top = left.astype(jnp.bfloat16)
-    rest = (left - top.astype(jnp.float32)).astype(jnp.bfloat16)
+    top, rest = halves(left)
     high = dot(jnp.concatenate([top, rest], axis=0), parts[0])
     return high[:outs] + (high[outs:] + dot(top, parts[1]))
 
@@ -103,10 +99,10 @@
     residual_ref,
     direction_ref,
     rz_ref,
-    image_out,
-    direction_out,
-    inner_out,
-    alpha_out,
+    image_hbm,
+    direction_hbm,
+    inner_hbm,
+    alpha_hbm,
     chol,
     chol_parts,
     inverse_parts,
@@ -139,6 +135,15 @@
     point_fwd,
     own_sems,
     share_sems,
+    image_out,
+    direction_out,
+    inner_out,
+    alpha_out,
+    out_sems,
+    square_buf,
+    square_all,
+    square_sems,
+    all_sems,
 ):
     me = lax.axis_index("rows")
     feat, local = points_ref.shape
@@ -234,13 +239,36 @@
 
     tiles = land // TILE
     groups = land // GROUP
-    rows_per = outs * tiles // n
-    for piece in range(n):
-        h, j = piece // tiles, piece % tiles
-        rs_send[piece, 0:rows_per] = proj[h * rows_per:(h + 1) * rows_per, j * TILE:(j + 1) * TILE]
-        rs_send[piece, rows_per:rows_per + 1] = own_square
-    send_all(lambda to: rs_send.at[to], rs_recv, rs_sems)
-    rs_recv[me, 0:rows_per + 1] = rs_send[me, 0:rows_per + 1]
+
+    base = (n - tiles) // 2
+    adds = (me >= base) & (me < base + tiles)
+    mine = me - base
+
+    def tile_to(q):
+        return remote(rs_send.at[q], rs_recv.at[me], rs_sems.at[0, q], rs_sems.at[1, me], base + q)
+
+    def each_tile(body):
+        def one(q, carry):
+            @pl.when(base + q != me)
+            def _():
+                body(q)
+
+            return carry
+
+        lax.fori_loop(0, tiles, one, 0)
+
+    for q in range(tiles):
+        rs_send[q] = proj[:, q * TILE:(q + 1) * TILE]
+    square_buf[me] = own_square
+    each_tile(lambda q: tile_to(q).start())
+
+    def square_to(to):
+        return remote(square_buf.at[me], square_buf.at[me], square_sems.at[0], square_sems.at[1 + me], to)
+
+    @pl.when(me != base)
+    def _():
+        square_to(base).start()
+
     own_side.start()
     for copy in own_left:
         copy.start()
@@ -276,7 +304,7 @@
                 on_col = jnp.sum(inverted[b], axis=0, keepdims=True)
                 change = on_row * off * on_col
             else:
-                change = dot_nn(dot_nn(inverted[b], off, HIGH), inverted[b], HIGH)
+                change = dot_square(dot_square(inverted[b], off), inverted[b])
             inverted[b] = inverted[b] - change
         size *= 2
     for b in range(share):
@@ -309,19 +337,35 @@
 
     own_slot, side_slot, across_slot = 2 * half - 1, 2 * half, 2 * half - 2
 
+    remote(points_ref, points.at[partner], own_sems.at[0], own_sems.at[1], partner).wait_recv()
+    side_aug[0:feat, :] = points[partner]
+    side_aug[feat:, :] = norm_rows(points[partner], True)
+    def total_to(to):
+        return remote(ag.at[mine], ag.at[mine], ag_sems.at[0, to], ag_sems.at[1, mine], to)
+
+    @pl.when(adds)
+    def _():
+        rs_recv[me] = rs_send[mine]
+        others(lambda src: remote(
+            rs_send.at[0], rs_recv.at[src], rs_sems.at[0, 0], rs_sems.at[1, src], src).wait_recv())
+        ag[mine] = jnp.sum(rs_recv[...], axis=0)
+        others(lambda to: total_to(to).start())
+
+    def all_square_to(to):
+        return remote(square_all, square_all, all_sems.at[0, to], all_sems.at[1, 0], to)
+
+    @pl.when(me == base)
+    def _():
+        others(lambda src: remote(
+            square_buf.at[src], square_buf.at[src], square_sems.at[0], square_sems.at[1 + src], src).wait_recv())
+        square_all[...] = jnp.sum(square_buf[...], axis=0)
+        others(lambda to: all_square_to(to).start())
+
+    if half > 1:
+        pass_on(1, 0)
     if keep:
         make_left(points_ref)
         make_block(own_slot, own_aug)
-    remote(points_ref, points.at[partner], own_sems.at[0], own_sems.at[1], partner).wait_recv()
-    side_aug[0:feat, :] = points[partner]
-    side_aug[feat:, :] = norm_rows(points[partner], True)
-    wait_all(lambda to: rs_send.at[to], rs_recv, rs_sems)
-    gathered = jnp.sum(rs_recv[:, 0:rows_per + 1], axis=0)
-    ag[me] = gathered[0:rows_per]
-    square = to_column(gathered[rows_per:rows_per + 1])
-    send_all(lambda to: ag.at[me], ag, ag_sems)
-    if half > 1:
-        pass_on(1, 0)
 
     other = inverse.at[pl.ds(share - first, share)]
     remote(other, other, share_sems.at[0], share_sems.at[1], partner).wait_recv()
@@ -329,14 +373,14 @@
         upper_block, lower_block = inverse[2 * b], inverse[2 * b + 1]
         at, end = b * GROUP, (b + 1) * GROUP
         off = chol[at + TILE:end, at:at + TILE]
-        change = dot_nn(dot_nn(lower_block, off, HIGH), upper_block, HIGH)
+        change = dot_square(dot_square(lower_block, off), upper_block)
         zero = jnp.zeros_like(upper_block)
         whole = jnp.concatenate(
             [jnp.concatenate([upper_block, zero], axis=1), jnp.concatenate([-change, lower_block], axis=1)], axis=0
         )
-        store_split(inverse_parts, (b,), whole)
+        store_pair(inverse_parts, (b,), whole)
         if b > 0:
-            store_split(chol_parts, (slice(at, end), slice(0, at)), chol[at:end, :at])
+            store_pair(chol_parts, (slice(at, end), slice(0, at)), chol[at:end, :at])
 
     def make_pair(k, slot):
         make_left(points.at[near(k)])
@@ -352,33 +396,37 @@
             make_pair(1, 0)
     if half > 2:
         pass_on(2, 0)
-    wait_all(lambda to: ag.at[me], ag, ag_sems)
-    for piece in range(n):
-        h, j = piece // tiles, piece % tiles
-        work[h * rows_per:(h + 1) * rows_per, j * TILE:(j + 1) * TILE] = ag[piece]
+    each_tile(lambda q: remote(ag.at[q], ag.at[q], ag_sems.at[0, me], ag_sems.at[1, q], base + q).wait_recv())
+    for q in range(tiles):
+        work[:, q * TILE:(q + 1) * TILE] = ag[q]
     pieces = [work[:, b * GROUP:(b + 1) * GROUP] for b in range(groups)]
 
     def block_parts(i, j):
         rows, cols = slice(i * GROUP, (i + 1) * GROUP), slice(j * GROUP, (j + 1) * GROUP)
-        return [chol_parts[term, rows, cols] for term in range(3)]
+        return [chol_parts[term, rows, cols] for term in range(2)]
 
     def inverse_of(b):
-        return [inverse_parts[term, b] for term in range(3)]
+        return [inverse_parts[term, b] for term in range(2)]
 
     for b in range(groups):
-        pieces[b] = dot_split(pieces[b], inverse_of(b), dot_nt)
+        pieces[b] = dot_pair(pieces[b], inverse_of(b), dot_nt)
         for i in range(b + 1, groups):
-            pieces[i] = pieces[i] - dot_split(pieces[b], block_parts(i, b), dot_nt)
+            pieces[i] = pieces[i] - dot_pair(pieces[b], block_parts(i, b), dot_nt)
     halfway = jnp.concatenate(pieces, axis=1)
     if half > 2:
         pass_on(2, 1)
     for b in reversed(range(groups)):
-        pieces[b] = dot_split(pieces[b], inverse_of(b), dot_nn)
+        pieces[b] = dot_pair(pieces[b], inverse_of(b), dot_nn)
         for j in reversed(range(b)):
-            pieces[j] = pieces[j] - dot_split(pieces[b], block_parts(b, j), dot_nn)
+            pieces[j] = pieces[j] - dot_pair(pieces[b], block_parts(b, j), dot_nn)
     coeffs = jnp.concatenate(pieces, axis=1)
 
     ridge = ridge_ref[...]
+    @pl.when(me != base)
+    def _():
+        all_square_to(base).wait_recv()
+
+    square = to_column(square_all[...])
     inner = (square - jnp.sum(halfway * halfway, axis=1, keepdims=True)) / ridge
     inner_out[...] = to_row(inner, TILE)[:, :outs]
     residual = residual_ref[...]
@@ -386,6 +434,16 @@
     direction_new = precond + (inner / to_column(rz_ref[...])) * direction_ref[...]
     direction_out[...] = direction_new
     dirs[me] = direction_new.astype(jnp.bfloat16)
+
+    def copy_out(at, src, dst):
+        return pltpu.make_async_copy(src, dst, out_sems.at[at])
+
+    direction_copy = copy_out(0, direction_out, direction_hbm)
+    inner_copy = copy_out(1, inner_out, inner_hbm)
+    image_copy = copy_out(2, image_out, image_hbm)
+    alpha_copy = copy_out(3, alpha_out, alpha_hbm)
+    direction_copy.start()
+    inner_copy.start()
 
     def dir_to(to):
         return remote(dirs.at[me], dirs.at[to], dir_sems.at[0, to], dir_sems.at[1, me], to)
@@ -521,8 +579,20 @@
     if keep:
         forward(across, across_slot, False)
 
-    drain(lambda to: rs_send.at[to], rs_recv, rs_sems)
-    drain(lambda to: ag.at[me], ag, ag_sems)
+    each_tile(lambda q: tile_to(q).wait_send())
+
+    @pl.when(me != base)
+    def _():
+        square_to(base).wait_send()
+
+    @pl.when(me == base)
+    def _():
+        others(lambda to: all_square_to(to).wait_send())
+
+    @pl.when(adds)
+    def _():
+        others(lambda to: total_to(to).wait_send())
+
     shared.wait_send()
     for copy in own_left:
         copy.wait_send()
@@ -549,13 +619,19 @@
         image_to(k, across).wait_recv()
         image = image + img_recv[k]
     image_out[...] = image
+    image_copy.start()
 
     wait_all(lambda to: curv_buf.at[me], curv_buf, curv_sems)
     alpha_out[...] = inner_out[...] / jnp.sum(curv_buf[...], axis=0)[:, :outs]
+    alpha_copy.start()
     drain(lambda to: curv_buf.at[me], curv_buf, curv_sems)
     side_send.wait_send()
     for k in range(half):
         image_to(k, across).wait_send()
+    direction_copy.wait()
+    inner_copy.wait()
+    image_copy.wait()
+    alpha_copy.wait()
 
 
 def finish(
@@ -587,13 +663,13 @@
         outs = residual.shape[0]
         keep = n <= STORED_BLOCKS
         half = n // 4
-        piece = outs * land // (TILE * n)
-        padded = -(-(piece + 1) // 8) * 8
+        tiles = land // TILE
         f32, bf16 = jnp.float32, jnp.bfloat16
         vmem = pl.BlockSpec(memory_space=pltpu.VMEM)
         wide = jax.ShapeDtypeStruct((outs, own), f32)
         thin = jax.ShapeDtypeStruct((1, outs), f32)
         dma = pltpu.SemaphoreType.DMA
+        anywhere = pl.BlockSpec(memory_space=pl.ANY)
         results = pl.pallas_call(
             functools.partial(kernel, n, keep),
             out_shape=(wide, wide, thin, thin),
@@ -606,21 +682,21 @@
                 vmem,
                 vmem,
             ],
-            out_specs=(vmem,) * 4,
+            out_specs=(anywhere,) * 4,
             scratch_shapes=[
                 pltpu.VMEM((land, land), f32),
-                pltpu.VMEM((3, land, land), bf16),
-                pltpu.VMEM((3, land // GROUP, GROUP, GROUP), bf16),
-                pltpu.VMEM((land // TILE, TILE, TILE), f32),
+                pltpu.VMEM((2, land, land), bf16),
+                pltpu.VMEM((2, land // GROUP, GROUP, GROUP), bf16),
+                pltpu.VMEM((tiles, TILE, TILE), f32),
                 pltpu.VMEM((n, feat, own), bf16),
                 pltpu.VMEM((feat + 16, own), bf16),
                 pltpu.VMEM((feat + 16, own), bf16),
                 pltpu.VMEM((feat + 16, own), bf16),
                 pltpu.VMEM((2, own, land), bf16),
                 pltpu.VMEM((2 * half + 1 if keep else 2, own, own), bf16),
-                pltpu.VMEM((n, padded, TILE), f32),
-                pltpu.VMEM((n, padded, TILE), f32),
-                pltpu.VMEM((n, piece, TILE), f32),
+                pltpu.VMEM((tiles, outs, TILE), f32),
+                pltpu.VMEM((n, outs, TILE), f32),
+                pltpu.VMEM((tiles, outs, TILE), f32),
                 pltpu.VMEM((outs, land), f32),
                 pltpu.VMEM((outs, land), f32),
                 pltpu.VMEM((n, outs, own), bf16),
@@ -640,9 +716,18 @@
                 dma((half, 2)),
                 dma((2,)),
                 dma((2,)),
+                pltpu.VMEM((outs, own), f32),
+                pltpu.VMEM((outs, own), f32),
+                pltpu.VMEM((1, outs), f32),
+                pltpu.VMEM((1, outs), f32),
+                dma((4,)),
+                pltpu.VMEM((n, 1, TILE), f32),
+                pltpu.VMEM((1, TILE), f32),
+                dma((1 + n,)),
+                dma((2, n)),
             ],
             compiler_params=pltpu.CompilerParams(
-                collective_id=0, has_side_effects=True, vmem_limit_bytes=62 * 1024 * 1024
+                collective_id=0, has_side_effects=True, vmem_limit_bytes=LIMIT * 1024 * 1024
             ),
             name="cg_step",
         )(points, landmarks, chol, ridge.reshape(1, 1), residual, direction, rz_prev.reshape(1, outs))

time: 38.9 us -> 37.8 us (0.972)
  Pallas kernels: 37.4 us -> 36.3 us
    pallas_call x1, Pallas kernels: 35.8 us -> 34.7 us  [local(): pl.pallas_call(functools.partial(kernel, n, keep), out_shape=(wide, wide,...]
where the time goes in v5:
time: 37.8 us; the launch traced here: 37.6 us
  Pallas kernels  36.3 us (96%)
  between operations  1.29 us (3%)
    pallas_call x1, Pallas kernels, local(): pl.pallas_call(functools.partial(kernel, n, keep), out_shape=(wide, wide,...  34.7 us
    pallas_call x1, Pallas kernels, local(): pl.pallas_call(finish, out_shape=(wide, wide, wide, thin), in_specs=[vmem...  1.54 us

profile of v5, /device:TPU:0, one launch (start us, length us, event | category | flops | bytes accessed | tf_op | source)
XLA Modules:
  0.0 37.6 jit_solution(13684311533253085286)
XLA Ops:
  1.3 34.7 %cg_step.1 = (f32[8,1024]{1,0:T(8,128)}, f32[8,1024]{1,0:T(8,128)}, f32[1,8]{1,0:T(1,128)}, f32[1,8]{1,0:T(1,128)}) custom-call(bf16[64,1024]{1,0:T(8,128)(2,1)} %points_ref.1, bf16[64,1024]{1,0:T(8,128)(2,1)} %landmarks_ref.1, f32[1024,1024]{1,0:T(8,128)} %chol_hbm.1, f32[1,1]{1,0:T(1,128)} %bitcast.3.ridge_ref, f32[8,1024]{1,0:T(8,128)} %residual_ref.3, ...), custom_call_target="tpu_custom_call" | custom-call | tf_op jit(solution)/shard_map/cg_step/pallas_call | solution.py:673
  36.0 1.5 %finish.1 = (f32[8,1024]{1,0:T(8,128)}, f32[8,1024]{1,0:T(8,128)}, f32[8,1024]{1,0:T(8,128)}, f32[1,8]{1,0:T(1,128)}) custom-call(f32[8,1024]{1,0:T(8,128)} %get-tuple-element.12.image_ref, f32[8,1024]{1,0:T(8,128)} %get-tuple-element.13.direction_ref, f32[1,8]{1,0:T(1,128)} %get-tuple-element.14.inner_ref, f32[1,8]{1,0:T(1,128)} %get-tuple-element.15.alpha_ref, ...), custom_call_target="tpu_custom_call" | custom-call | tf_op jit(solution)/shard_map/finish/pallas_call | solution.py:734

commit v6 on v5

--- a/solution.py
+++ b/solution.py
@@ -188,10 +188,6 @@
     chol_copy = pltpu.make_async_copy(chol_hbm, chol, chol_sem)
     chol_copy.start()
 
-    barrier = pltpu.get_barrier_semaphore()
-    others(lambda to: pl.semaphore_signal(
-        barrier, inc=1, device_id={"rows": to}, device_id_type=pl.DeviceIdType.MESH))
-
     upper = pos // half
     partner = row_of(pos, 1)
     left = row_of(pos - 1, 0)
@@ -199,6 +195,24 @@
     across = row_of(pos + half, upper)
     taker = row_of(pos + half, 1 - upper)
 
+    tiles = land // TILE
+    base = (n - tiles) // 2
+    adds = (me >= base) & (me < base + tiles)
+    mine = me - base
+
+    barrier = pltpu.get_barrier_semaphore()
+
+    def greet(to):
+        pl.semaphore_signal(barrier, inc=1, device_id={"rows": to}, device_id_type=pl.DeviceIdType.MESH)
+
+    greet(partner)
+    greet(row_of(pos + 1, 0))
+    greet(row_of(pos + 1, 1))
+
+    @pl.when(adds)
+    def _():
+        others(greet)
+
     def near(k):
         return row_of(pos + k, 0)
 
@@ -222,27 +236,18 @@
 
     proj[...] = jnp.zeros_like(proj)
 
-    def project(i, carry):
-        at = pl.multiple_of(i * CHUNK, CHUNK)
+    for at in range(0, local, CHUNK):
         values = entries(own_aug, at, col_aug)
         top = values.astype(jnp.bfloat16)
         cross[0, pl.ds(at, CHUNK), :] = top
         cross[1, pl.ds(at, CHUNK), :] = (values - top.astype(jnp.float32)).astype(jnp.bfloat16)
         parts = [cross[term, pl.ds(at, CHUNK), :] for term in range(2)]
         proj[...] += dot_pair(residual_ref[:, pl.ds(at, CHUNK)], parts, dot_nn)
-        return carry
-
-    lax.fori_loop(0, local // CHUNK, project, 0)
     own_square = to_row(jnp.sum(residual_ref[...] * residual_ref[...], axis=1, keepdims=True), TILE)
 
-    pl.semaphore_wait(barrier, n - 1)
-
-    tiles = land // TILE
+    pl.semaphore_wait(barrier, tiles + 3 - jnp.where(adds, 1, 0))
+
     groups = land // GROUP
-
-    base = (n - tiles) // 2
-    adds = (me >= base) & (me < base + tiles)
-    mine = me - base
 
     def tile_to(q):
         return remote(rs_send.at[q], rs_recv.at[me], rs_sems.at[0, q], rs_sems.at[1, me], base + q)
@@ -340,32 +345,15 @@
     remote(points_ref, points.at[partner], own_sems.at[0], own_sems.at[1], partner).wait_recv()
     side_aug[0:feat, :] = points[partner]
     side_aug[feat:, :] = norm_rows(points[partner], True)
-    def total_to(to):
-        return remote(ag.at[mine], ag.at[mine], ag_sems.at[0, to], ag_sems.at[1, mine], to)
-
-    @pl.when(adds)
-    def _():
-        rs_recv[me] = rs_send[mine]
-        others(lambda src: remote(
-            rs_send.at[0], rs_recv.at[src], rs_sems.at[0, 0], rs_sems.at[1, src], src).wait_recv())
-        ag[mine] = jnp.sum(rs_recv[...], axis=0)
-        others(lambda to: total_to(to).start())
-
-    def all_square_to(to):
-        return remote(square_all, square_all, all_sems.at[0, to], all_sems.at[1, 0], to)
-
-    @pl.when(me == base)
-    def _():
-        others(lambda src: remote(
-            square_buf.at[src], square_buf.at[src], square_sems.at[0], square_sems.at[1 + src], src).wait_recv())
-        square_all[...] = jnp.sum(square_buf[...], axis=0)
-        others(lambda to: all_square_to(to).start())
-
-    if half > 1:
-        pass_on(1, 0)
     if keep:
         make_left(points_ref)
         make_block(own_slot, own_aug)
+        make_left(points.at[partner])
+        make_block(side_slot, own_aug)
+    if half > 1:
+        @pl.when(jnp.logical_not(adds))
+        def _():
+            pass_on(1, 0)
 
     other = inverse.at[pl.ds(share - first, share)]
     remote(other, other, share_sems.at[0], share_sems.at[1], partner).wait_recv()
@@ -387,15 +375,33 @@
         make_block(slot, own_aug)
         make_block(slot + 1, side_aug)
 
+    def total_to(to):
+        return remote(ag.at[mine], ag.at[mine], ag_sems.at[0, to], ag_sems.at[1, mine], to)
+
+    @pl.when(adds)
+    def _():
+        rs_recv[me] = rs_send[mine]
+        others(lambda src: remote(
+            rs_send.at[0], rs_recv.at[src], rs_sems.at[0, 0], rs_sems.at[1, src], src).wait_recv())
+        ag[mine] = jnp.sum(rs_recv[...], axis=0)
+        others(lambda to: total_to(to).start())
+        if half > 1:
+            pass_on(1, 0)
+
+    def all_square_to(to):
+        return remote(square_all, square_all, all_sems.at[0, to], all_sems.at[1, 0], to)
+
+    @pl.when(me == base)
+    def _():
+        others(lambda src: remote(
+            square_buf.at[src], square_buf.at[src], square_sems.at[0], square_sems.at[1 + src], src).wait_recv())
+        square_all[...] = jnp.sum(square_buf[...], axis=0)
+        others(lambda to: all_square_to(to).start())
+
     if half > 1:
         pass_on(1, 1)
-    if keep:
-        make_left(points.at[partner])
-        make_block(side_slot, own_aug)
-        if half > 1:
-            make_pair(1, 0)
-    if half > 2:
-        pass_on(2, 0)
+    if keep and half > 1:
+        make_pair(1, 0)
     each_tile(lambda q: remote(ag.at[q], ag.at[q], ag_sems.at[0, me], ag_sems.at[1, q], base + q).wait_recv())
     for q in range(tiles):
         work[:, q * TILE:(q + 1) * TILE] = ag[q]
@@ -414,12 +420,14 @@
             pieces[i] = pieces[i] - dot_pair(pieces[b], block_parts(i, b), dot_nt)
     halfway = jnp.concatenate(pieces, axis=1)
     if half > 2:
-        pass_on(2, 1)
+        pass_on(2, 0)
     for b in reversed(range(groups)):
         pieces[b] = dot_pair(pieces[b], inverse_of(b), dot_nn)
         for j in reversed(range(b)):
             pieces[j] = pieces[j] - dot_pair(pieces[b], block_parts(b, j), dot_nn)
     coeffs = jnp.concatenate(pieces, axis=1)
+    if half > 2:
+        pass_on(2, 1)
 
     ridge = ridge_ref[...]
     @pl.when(me != base)
@@ -457,9 +465,6 @@
     send_dir(taker)
     lax.fori_loop(1, half, lambda k, carry: (send_dir(back(half - k)), carry)[1], 0)
     send_dir(partner)
-    if keep and half > 3:
-        pass_on(3, 0)
-
     def wait_across():
         for h in range(2):
             hop(0, h, points.at[across], across, left).wait_recv()
@@ -494,32 +499,32 @@
         acc[3] += total * dirs[owner].astype(jnp.float32)
 
     if keep:
-        for k in range(2, half):
+        if half > 2:
+            make_pair(2, 2)
+        if half > 3:
+            pass_on(3, 0)
+        wait_dir(partner)
+        at_own(own_slot)
+        at_side(side_slot)
+        if half > 3:
+            pass_on(3, 1)
+
+        def ahead(k, carry):
+            wait_dir(near(k))
+            forward(near(k), 2 * (k - 1), True)
+            return carry
+
+        lax.fori_loop(1, min(half, early), ahead, 0)
+        low = dirs[partner].astype(jnp.float32)
+        acc[3] = direction_out[...] * acc[1] + low * acc[2]
+        for k in range(early, half):
             if k > 3:
                 pass_on(k, 0)
                 pass_on(k, 1)
             make_pair(k, 2 * (k - 1))
-            if k == 2 and half > 3:
-                pass_on(3, 1)
-            if k == 2:
-                wait_dir(partner)
-            if k >= early:
-                sent = backward(k - 1, near(k), 2 * (k - 1), True)
-                wait_dir(near(k))
-                terms_behind(sent, near(k))
-        if half < 3:
-            wait_dir(partner)
-        at_own(own_slot)
-        at_side(side_slot)
-
-        def ahead(k, carry):
+            sent = backward(k - 1, near(k), 2 * (k - 1), True)
             wait_dir(near(k))
-            forward(near(k), 2 * (k - 1), True)
-            return carry
-
-        lax.fori_loop(1, min(half, early), ahead, 0)
-        low = dirs[partner].astype(jnp.float32)
-        acc[3] += direction_out[...] * acc[1] + low * acc[2]
+            terms_behind(sent, near(k))
         wait_across()
         make_left(points.at[across])
         make_block(across_slot, own_aug)

time: 37.8 us -> 37.9 us (level)
  no operation moved by 1% of the time
where the time goes in v6:
time: 37.9 us; the launch traced here: 37.7 us
  Pallas kernels  36.4 us (96%)
  between operations  1.29 us (3%)
    pallas_call x1, Pallas kernels, local(): pl.pallas_call(functools.partial(kernel, n, keep), out_shape=(wide, wide,...  34.8 us
    pallas_call x1, Pallas kernels, local(): pl.pallas_call(finish, out_shape=(wide, wide, wide, thin), in_specs=[vmem...  1.54 us

profile of v6, /device:TPU:0, one launch (start us, length us, event | category | flops | bytes accessed | tf_op | source)
XLA Modules:
  0.0 37.7 jit_solution(10880308210529213218)
XLA Ops:
  1.3 34.8 %cg_step.1 = (f32[8,1024]{1,0:T(8,128)}, f32[8,1024]{1,0:T(8,128)}, f32[1,8]{1,0:T(1,128)}, f32[1,8]{1,0:T(1,128)}) custom-call(bf16[64,1024]{1,0:T(8,128)(2,1)} %points_ref.1, bf16[64,1024]{1,0:T(8,128)(2,1)} %landmarks_ref.1, f32[1024,1024]{1,0:T(8,128)} %chol_hbm.1, f32[1,1]{1,0:T(1,128)} %bitcast.3.ridge_ref, f32[8,1024]{1,0:T(8,128)} %residual_ref.3, ...), custom_call_target="tpu_custom_call" | custom-call | tf_op jit(solution)/shard_map/cg_step/pallas_call | solution.py:678
  36.1 1.5 %finish.1 = (f32[8,1024]{1,0:T(8,128)}, f32[8,1024]{1,0:T(8,128)}, f32[8,1024]{1,0:T(8,128)}, f32[1,8]{1,0:T(1,128)}) custom-call(f32[8,1024]{1,0:T(8,128)} %get-tuple-element.12.image_ref, f32[8,1024]{1,0:T(8,128)} %get-tuple-element.13.direction_ref, f32[1,8]{1,0:T(1,128)} %get-tuple-element.14.inner_ref, f32[1,8]{1,0:T(1,128)} %get-tuple-element.15.alpha_ref, ...), custom_call_target="tpu_custom_call" | custom-call | tf_op jit(solution)/shard_map/finish/pallas_call | solution.py:739

commit v7 on v5

--- a/solution.py
+++ b/solution.py
@@ -188,10 +188,6 @@
     chol_copy = pltpu.make_async_copy(chol_hbm, chol, chol_sem)
     chol_copy.start()
 
-    barrier = pltpu.get_barrier_semaphore()
-    others(lambda to: pl.semaphore_signal(
-        barrier, inc=1, device_id={"rows": to}, device_id_type=pl.DeviceIdType.MESH))
-
     upper = pos // half
     partner = row_of(pos, 1)
     left = row_of(pos - 1, 0)
@@ -199,6 +195,24 @@
     across = row_of(pos + half, upper)
     taker = row_of(pos + half, 1 - upper)
 
+    tiles = land // TILE
+    base = (n - tiles) // 2
+    adds = (me >= base) & (me < base + tiles)
+    mine = me - base
+
+    barrier = pltpu.get_barrier_semaphore()
+
+    def greet(to):
+        pl.semaphore_signal(barrier, inc=1, device_id={"rows": to}, device_id_type=pl.DeviceIdType.MESH)
+
+    greet(partner)
+    greet(row_of(pos + 1, 0))
+    greet(row_of(pos + 1, 1))
+
+    @pl.when(adds)
+    def _():
+        others(greet)
+
     def near(k):
         return row_of(pos + k, 0)
 
@@ -222,27 +236,19 @@
 
     proj[...] = jnp.zeros_like(proj)
 
-    def project(i, carry):
-        at = pl.multiple_of(i * CHUNK, CHUNK)
+    for at in range(0, local, CHUNK):
         values = entries(own_aug, at, col_aug)
         top = values.astype(jnp.bfloat16)
         cross[0, pl.ds(at, CHUNK), :] = top
         cross[1, pl.ds(at, CHUNK), :] = (values - top.astype(jnp.float32)).astype(jnp.bfloat16)
         parts = [cross[term, pl.ds(at, CHUNK), :] for term in range(2)]
         proj[...] += dot_pair(residual_ref[:, pl.ds(at, CHUNK)], parts, dot_nn)
-        return carry
-
-    lax.fori_loop(0, local // CHUNK, project, 0)
+
     own_square = to_row(jnp.sum(residual_ref[...] * residual_ref[...], axis=1, keepdims=True), TILE)
 
-    pl.semaphore_wait(barrier, n - 1)
-
-    tiles = land // TILE
+    pl.semaphore_wait(barrier, tiles + 3 - jnp.where(adds, 1, 0))
+
     groups = land // GROUP
-
-    base = (n - tiles) // 2
-    adds = (me >= base) & (me < base + tiles)
-    mine = me - base
 
     def tile_to(q):
         return remote(rs_send.at[q], rs_recv.at[me], rs_sems.at[0, q], rs_sems.at[1, me], base + q)

time: 37.8 us -> 37.1 us (0.981)
  Pallas kernels: 36.3 us -> 35.6 us
    pallas_call x1, Pallas kernels: 34.7 us -> 34 us  [local(): pl.pallas_call(functools.partial(kernel, n, keep), out_shape=(wide, wide,...]
where the time goes in v7:
time: 37.1 us; the launch traced here: 36.9 us
  Pallas kernels  35.6 us (96%)
  between operations  1.29 us (3%)
    pallas_call x1, Pallas kernels, local(): pl.pallas_call(functools.partial(kernel, n, keep), out_shape=(wide, wide,...  34 us
    pallas_call x1, Pallas kernels, local(): pl.pallas_call(finish, out_shape=(wide, wide, wide, thin), in_specs=[vmem...  1.54 us

profile of v7, /device:TPU:0, one launch (start us, length us, event | category | flops | bytes accessed | tf_op | source)
XLA Modules:
  0.0 36.9 jit_solution(8007672485806355163)
XLA Ops:
  1.3 34.0 %cg_step.1 = (f32[8,1024]{1,0:T(8,128)}, f32[8,1024]{1,0:T(8,128)}, f32[1,8]{1,0:T(1,128)}, f32[1,8]{1,0:T(1,128)}) custom-call(bf16[64,1024]{1,0:T(8,128)(2,1)} %points_ref.1, bf16[64,1024]{1,0:T(8,128)(2,1)} %landmarks_ref.1, f32[1024,1024]{1,0:T(8,128)} %chol_hbm.1, f32[1,1]{1,0:T(1,128)} %bitcast.3.ridge_ref, f32[8,1024]{1,0:T(8,128)} %residual_ref.3, ...), custom_call_target="tpu_custom_call" | custom-call | tf_op jit(solution)/shard_map/cg_step/pallas_call | solution.py:679
  35.3 1.5 %finish.1 = (f32[8,1024]{1,0:T(8,128)}, f32[8,1024]{1,0:T(8,128)}, f32[8,1024]{1,0:T(8,128)}, f32[1,8]{1,0:T(1,128)}) custom-call(f32[8,1024]{1,0:T(8,128)} %get-tuple-element.12.image_ref, f32[8,1024]{1,0:T(8,128)} %get-tuple-element.13.direction_ref, f32[1,8]{1,0:T(1,128)} %get-tuple-element.14.inner_ref, f32[1,8]{1,0:T(1,128)} %get-tuple-element.15.alpha_ref, ...), custom_call_target="tpu_custom_call" | custom-call | tf_op jit(solution)/shard_map/finish/pallas_call | solution.py:740
